TPU v7x, 256 devices: a whole 4x4x8 slice. The times are simulated.
256 devices in a mesh: row: 16 (over x_hi, y, core), col: 16 (over z, x_lo).
Axes of the slice: x: 4 (x_hi: 2, x_lo: 2; x = x_hi * 2 + x_lo), y: 4, z: 8, core: 2. Of those that a mesh axis runs over, the one named last changes fastest.
Arguments:
- train_grads: bfloat16 [8192, 8192], P('row', 'col'), may hold values from -16 to 16
- query_grads: bfloat16 [8192, 8192], P('col', 'row'), may hold values from -6 to 6
Outputs:
- scores: float32 [8192, 8192], P('row', 'col')
All inputs are finite; a program needn't handle non-finite values.
Results may differ from a plain program's by a relative error of at most 0.0081.
Values may be sent and summed in bfloat16 or wider, within the bound.
No kernel may reach another device: no remote copies, remote signals or barrier semaphores. Data moves between devices by JAX's collectives and lax.ppermute only.
A program may use at most 128 MiB of HBM per device.

v0:
```python
import math

import jax
import jax.numpy as jnp
from jax import lax
from jax.experimental import pallas as pl
from jax.experimental.pallas import tpu as pltpu
from jax.sharding import Mesh
from jax.sharding import PartitionSpec as P


PROJ = 64
LAYERS = 2
ROW = ("xh", "y", "co")
COL = ("zh", "zl", "xl")
Z = ("zh", "zl")
DAMPING = 0.1
SWAP = [(0, 1), (1, 0)]
F32 = jnp.float32
BF16 = jnp.bfloat16
VMEM = pl.BlockSpec(memory_space=pltpu.VMEM)
SMEM = pl.BlockSpec(memory_space=pltpu.SMEM)
ANY = pl.BlockSpec(memory_space=pl.ANY)
HBM = pl.BlockSpec(memory_space=pltpu.HBM)


def ring(value, axes, size):
    pairs = []
    for core, step in ((0, 1), (1, -1)):
        for n in range(size):
            to = (n + step) % size
            pair = (core * size + n, core * size + to) if axes[0] == "co" else (2 * n + core, 2 * to + core)
            pairs.append(pair)
    return lax.ppermute(value, axes, pairs)


def swap(value, axis):
    return lax.ppermute(value, axis, SWAP)


def iota(shape, dim):
    return lax.broadcasted_iota(jnp.int32, shape, dim)


def invert(mats):
    shape = (PROJ, PROJ)
    rows, cols, lane = iota(shape, 0), iota(shape, 1), iota((1, PROJ), 1)

    def at(mask, value, axis=1):
        return jnp.sum(jnp.where(mask, value, 0.0), axis=axis, keepdims=True)

    def step(t, mats):
        k = 2 * t
        col0, col1, row0, row1 = cols == k, cols == k + 1, rows == k, rows == k + 1
        lane0, lane1 = lane == k, lane == k + 1
        out = []
        for a in mats:
            c0, c1 = at(col0, a), at(col1, a)
            r0, r1 = at(row0, a, 0), at(row1, a, 0)
            p, q, u, v = at(lane0, r0), at(lane1, r0), at(lane0, r1), at(lane1, r1)
            d = 1.0 / (p * v - q * u)
            r0 = jnp.where(lane0, 1.0, jnp.where(lane1, 0.0, r0))
            r1 = jnp.where(lane1, 1.0, jnp.where(lane0, 0.0, r1))
            n0 = (v * d) * r0 - (q * d) * r1
            n1 = (p * d) * r1 - (u * d) * r0
            rest = jnp.where(col0 | col1, 0.0, a) - c0 * n0 - c1 * n1
            out.append(jnp.where(row0, n0, jnp.where(row1, n1, rest)))
        return tuple(out)

    return lax.fori_loop(0, PROJ // 2, step, tuple(mats))


def inverse_kernel(count, factor_ref, out_ref):
    rows, cols = iota((PROJ, PROJ), 0), iota((PROJ, PROJ), 1)
    mats = []
    for n in range(2):
        factor = factor_ref[n] * (1.0 / count)
        diagonal = jnp.where(rows == cols, factor, 0.0)
        trace = jnp.sum(jnp.sum(diagonal, axis=1, keepdims=True), axis=0, keepdims=True)
        mats.append(factor + jnp.where(rows == cols, DAMPING * (trace / PROJ), 0.0))
    for n, inverse in enumerate(invert(mats)):
        out_ref[n] = inverse.astype(BF16)


def inverses(factors, count):
    return pl.pallas_call(
        lambda *refs: inverse_kernel(count, *refs),
        out_shape=jax.ShapeDtypeStruct((2, PROJ, PROJ), BF16),
        in_specs=[VMEM],
        out_specs=VMEM,
        compiler_params=pltpu.CompilerParams(vmem_limit_bytes=8 << 20),
        cost_estimate=pl.CostEstimate(flops=10**8, bytes_accessed=1 << 20, transcendentals=0),
        name="inverses",
    )(factors)


def expand(inverse_ref, wide_in_ref, wide_out_ref):
    r, i = iota((256, PROJ), 0), iota((256, PROJ), 1)
    pick_in = (i == (r // 32) * 8 + r % 8).astype(BF16)
    j, c = iota((PROJ, 256), 0), iota((PROJ, 256), 1)
    spread_in = (c % PROJ == j).astype(BF16)
    r, c = iota((256, 256), 0), iota((256, 256), 1)
    part = jnp.dot(pick_in, inverse_ref[0], preferred_element_type=F32).astype(BF16)
    part = jnp.dot(part, spread_in, preferred_element_type=F32)
    wide_in_ref[...] = jnp.where((r // 8) % 4 == c // PROJ, part, 0.0).astype(BF16)
    r, o = iota((512, PROJ), 0), iota((512, PROJ), 1)
    pick_out = (o == r // 8).astype(BF16)
    o, c = iota((PROJ, 512), 0), iota((PROJ, 512), 1)
    spread_out = (o == c // 8).astype(BF16)
    r, c = iota((512, 512), 0), iota((512, 512), 1)
    part = jnp.dot(pick_out, inverse_ref[1], preferred_element_type=F32).astype(BF16)
    part = jnp.dot(part, spread_out, preferred_element_type=F32)
    wide_out_ref[...] = jnp.where(r % 8 == c % 8, part, 0.0).astype(BF16)


def fetch_queries(near, far, use_near, query_buf, query_sem):
    copies = [
        [pltpu.make_async_copy(r, query_buf.at[n], query_sem.at[n]) for n, r in enumerate(refs)]
        for refs in (near, far)
    ]

    @pl.when(use_near)
    def _():
        start_all(copies[0])

    @pl.when(jnp.logical_not(use_near))
    def _():
        start_all(copies[1])

    return copies[0]


def condition_layer(places, me, copies, query_buf, half_ref, wide_in_ref, wide_out_ref, store):
    y, co = (me // 2) % 4, me % 2
    toward = 2 * co - 1
    width = half_ref.shape[-1]
    for n, (dy, along, dco) in enumerate(places):
        copies[n].wait()
        block = ((y + dy + along * toward + 4) % 4) * 2 + jnp.bitwise_xor(co, dco)
        for part in range(2):
            half = jnp.dot(
                wide_in_ref[...],
                query_buf[n, part * 256 : (part + 1) * 256, :],
                preferred_element_type=F32,
            ).astype(BF16)
            start = pl.multiple_of((block * 2 + part) * 32, 32)
            half_ref[:, pl.ds(start, 32), :] = half.reshape(8, 32, width)

    @pl.loop(0, 4)
    def _(k):
        both = [
            jnp.dot(wide_out_ref[...], half_ref[2 * k + g], preferred_element_type=F32)
            .reshape(PROJ, 8, width)
            for g in range(2)
        ]
        store(k, pl.multiple_of(16 * k, 16), jnp.concatenate(both, axis=1).astype(BF16))


def first_kernel(places, me_row_ref, me_col_ref, inverse_ref, *refs):
    near, far = refs[:8], refs[8:16]
    out_ref, query_buf, half_ref, cond_ref, wide_in_ref, wide_out_ref, query_sem, out_sem = refs[16:]
    me = me_row_ref[0]
    layer = (me_col_ref[0] // 8) % 2
    copies = fetch_queries(near, far, me // 8 == layer, query_buf, query_sem)
    expand(inverse_ref, wide_in_ref, wide_out_ref)

    def out_copy(k, start):
        rows = pl.ds(start, 16)
        return pltpu.make_async_copy(cond_ref.at[:, rows, :], out_ref.at[:, rows, :], out_sem.at[k])

    def store(k, start, value):
        cond_ref[:, pl.ds(start, 16), :] = value
        out_copy(k, start).start()

    condition_layer(places, me, copies, query_buf, half_ref, wide_in_ref, wide_out_ref, store)
    for k in range(4):
        out_copy(k, 16 * k).wait()


def condition_first(me_row, me_col, inverse, near, far, places):
    width = near[0].shape[-1]
    return pl.pallas_call(
        lambda *refs: first_kernel(places, *refs),
        out_shape=jax.ShapeDtypeStruct((PROJ, PROJ, width), BF16),
        in_specs=[SMEM, SMEM, VMEM] + [ANY] * 16,
        out_specs=HBM,
        scratch_shapes=[
            pltpu.VMEM((8, 512, width), BF16),
            pltpu.VMEM((8, 512, width), BF16),
            pltpu.VMEM((PROJ, PROJ, width), BF16),
            pltpu.VMEM((256, 256), BF16),
            pltpu.VMEM((512, 512), BF16),
            pltpu.SemaphoreType.DMA((8,)),
            pltpu.SemaphoreType.DMA((4,)),
        ],
        compiler_params=pltpu.CompilerParams(vmem_limit_bytes=20 << 20),
        cost_estimate=pl.CostEstimate(flops=3 * 10**9, bytes_accessed=8 << 20, transcendentals=0),
        name="condition_first",
    )(me_row, me_col, inverse, *near, *far)


def input_kernel(x_ref, out_ref):
    x = x_ref[...]
    gram = lax.dot_general(x, x, (((0,), (0,)), ((), ())), preferred_element_type=F32)
    gram = jnp.where(iota(gram.shape, 0) // PROJ == iota(gram.shape, 1) // PROJ, gram, 0.0)
    rows = jnp.sum(gram.reshape(8, PROJ, 512), axis=0)
    fold = rows[:, :128] + rows[:, 128:256] + rows[:, 256:384] + rows[:, 384:]
    out_ref[...] = fold[:, :PROJ] + fold[:, PROJ:]


def input_factor(train):
    return pl.pallas_call(
        input_kernel,
        out_shape=jax.ShapeDtypeStruct((PROJ, PROJ), F32),
        in_specs=[VMEM],
        out_specs=VMEM,
        compiler_params=pltpu.CompilerParams(vmem_limit_bytes=8 << 20),
        cost_estimate=pl.CostEstimate(flops=3 * 10**8, bytes_accessed=1 << 20, transcendentals=0),
        name="input_factor",
    )(train)


def terms_kernel(x_ref, input_ref, out_ref, side_ref, sum_ref):
    blocks, count, _ = x_ref.shape
    for b in range(blocks):
        turned = x_ref[b].astype(F32).T.astype(BF16).reshape(8, 4, 16, count)
        parts = [turned[:, g].reshape(128, count) for g in range(4)]
        side_ref[b * 128 : (b + 1) * 128, :] = jnp.concatenate(parts, axis=1)
    for b in range(blocks):
        gram = lax.dot_general(
            side_ref[b * 128 : (b + 1) * 128, :],
            side_ref[...],
            (((1,), (1,)), ((), ())),
            preferred_element_type=F32,
        )
        gram = jnp.where(iota(gram.shape, 0) % 16 == iota(gram.shape, 1) % 16, gram, 0.0)
        sum_ref[8 * b : 8 * b + 8, :] = jnp.sum(gram.reshape(8, 16, 1024), axis=1)
    ones = (iota((1024, PROJ), 0) // 16 == iota((1024, PROJ), 1)).astype(BF16)
    rest = sum_ref[...]
    total = jnp.zeros((PROJ, PROJ), F32)
    for _ in range(3):
        part = rest.astype(BF16)
        total += jnp.dot(part, ones, preferred_element_type=F32)
        rest = rest - part.astype(F32)
    out_ref[0] = input_ref[...]
    out_ref[1] = total


def factor_terms(blocks, input_term):
    count = blocks.shape[1]
    return pl.pallas_call(
        terms_kernel,
        out_shape=jax.ShapeDtypeStruct((2, PROJ, PROJ), F32),
        in_specs=[VMEM, VMEM],
        out_specs=VMEM,
        scratch_shapes=[pltpu.VMEM((1024, 4 * count), BF16), pltpu.VMEM((PROJ, 1024), F32)],
        compiler_params=pltpu.CompilerParams(vmem_limit_bytes=12 << 20),
        cost_estimate=pl.CostEstimate(flops=6 * 10**8, bytes_accessed=1 << 20, transcendentals=0),
        name="factor_terms",
    )(blocks, input_term)


def column_of(me, k, other):
    toward = jnp.where((me // 16) % 2 == 0, -k, k)
    return ((me // 2 + toward) % 8) * 2 + jnp.bitwise_xor(me % 2, other)


def start_all(copies):
    for copy in copies:
        copy.start()
    return copies


def main_kernel(places, own_places, me_row_ref, me_col_ref, inverse_ref, first_ref, *refs):
    near, far, theirs_refs, refs = refs[:8], refs[8:16], refs[16:22], refs[22:]
    own_refs, refs = refs[: len(own_places)], refs[len(own_places) :]
    out_ref, own_ref, late_ref, query_buf, half_ref, cond_ref, sum_ref, wide_in_ref, wide_out_ref = refs[:9]
    theirs_buf, own_buf, query_sem, theirs_sem, own_sem, late_sem, first_sem = refs[9:]

    me = me_row_ref[0]
    layer = (me_col_ref[0] // 8) % 2
    query_copies = fetch_queries(near, far, me // 8 != layer, query_buf, query_sem)
    first_start = pl.multiple_of(layer * PROJ, PROJ)
    first_copy = pltpu.make_async_copy(first_ref, cond_ref.at[pl.ds(first_start, PROJ)], first_sem.at[0])
    first_copy.start()
    theirs_copies = start_all(
        [pltpu.make_async_copy(r, theirs_buf.at[n], theirs_sem.at[n]) for n, r in enumerate(theirs_refs)]
    )
    own_copies = start_all(
        [
            pltpu.make_async_copy(r, own_buf.at[pl.ds(first * 512, slots * 512)], own_sem.at[first])
            for r, (first, slots) in zip(own_refs, own_places)
        ]
    )
    expand(inverse_ref, wide_in_ref, wide_out_ref)
    width = half_ref.shape[-1]
    second_start = pl.multiple_of((1 - layer) * PROJ, PROJ)

    def store(k, start, value):
        cond_ref[pl.ds(second_start, PROJ), pl.ds(start, 16), :] = value

    condition_layer(places, me, query_copies, query_buf, half_ref, wide_in_ref, wide_out_ref, store)
    first_copy.wait()

    me = me_col_ref[0]
    late_copies = start_all(
        [
            pltpu.make_async_copy(
                cond_ref.at[pl.ds(column_of(me, 3 + n // 2, n % 2) * 8, 8)], late_ref.at[n], late_sem.at[n]
            )
            for n in range(4)
        ]
    )

    def cond_of(k, other):
        return cond_ref[pl.ds(column_of(me, k, other) * 8, 8)].reshape(512, width)

    for n in range(6):
        theirs_copies[n].wait()
        part = jnp.dot(theirs_buf[n], cond_of(1 + n // 2, n % 2), preferred_element_type=F32)
        sum_ref[...] = part if n == 0 else sum_ref[...] + part
    out_ref[...] = sum_ref[...].astype(BF16)
    waits = {first: copy for copy, (first, _) in zip(own_copies, own_places)}
    for n in range(6):
        if n in waits:
            waits[n].wait()
        part = jnp.dot(
            own_buf[n * 512 : (n + 1) * 512, :], cond_of(n // 2, n % 2), preferred_element_type=F32
        )
        own_ref[...] = part if n == 0 else own_ref[...] + part
    for copy in late_copies:
        copy.wait()


def condition_and_score(me_row, me_col, inverse, first, near, far, places, theirs, own, own_places):
    width = near[0].shape[-1]
    return pl.pallas_call(
        lambda *refs: main_kernel(places, own_places, *refs),
        out_shape=(
            jax.ShapeDtypeStruct((512, width), BF16),
            jax.ShapeDtypeStruct((512, width), F32),
            jax.ShapeDtypeStruct((4, 8, PROJ, width), BF16),
        ),
        in_specs=[SMEM, SMEM, VMEM, HBM] + [ANY] * (16 + len(theirs) + len(own)),
        out_specs=(VMEM, VMEM, HBM),
        scratch_shapes=[
            pltpu.VMEM((8, 512, width), BF16),
            pltpu.VMEM((8, 512, width), BF16),
            pltpu.VMEM((LAYERS * PROJ, PROJ, width), BF16),
            pltpu.VMEM((512, width), F32),
            pltpu.VMEM((256, 256), BF16),
            pltpu.VMEM((512, 512), BF16),
            pltpu.VMEM((6, 512, 512), BF16),
            pltpu.VMEM((6 * 512, 512), BF16),
            pltpu.SemaphoreType.DMA((8,)),
            pltpu.SemaphoreType.DMA((6,)),
            pltpu.SemaphoreType.DMA((6,)),
            pltpu.SemaphoreType.DMA((4,)),
            pltpu.SemaphoreType.DMA((1,)),
        ],
        compiler_params=pltpu.CompilerParams(vmem_limit_bytes=34 << 20),
        cost_estimate=pl.CostEstimate(flops=6 * 10**9, bytes_accessed=18 << 20, transcendentals=0),
        name="condition_and_score",
    )(me_row, me_col, inverse, first, *near, *far, *theirs, *own)


def own_kernel(total_ref, cond_ref, near_ref, far_ref, out_ref):
    total = total_ref[...]
    for n in range(4):
        ref = (near_ref, far_ref)[n // 2]
        rows = ref[n % 2 * 512 : (n % 2 + 1) * 512, :]
        total += jnp.dot(
            rows, cond_ref[n].reshape(512, cond_ref.shape[-1]), preferred_element_type=F32
        )
    out_ref[...] = total


def score_own(total, cond, near, far):
    return pl.pallas_call(
        own_kernel,
        out_shape=jax.ShapeDtypeStruct(total.shape, F32),
        in_specs=[VMEM] * 4,
        out_specs=VMEM,
        compiler_params=pltpu.CompilerParams(vmem_limit_bytes=12 << 20),
        cost_estimate=pl.CostEstimate(flops=10**9, bytes_accessed=5 << 20, transcendentals=0),
        name="score_own",
    )(total, cond, near, far)


def all_of(value, axis, size):
    total = value
    for k in range(1, size):
        total = total + lax.ppermute(value, axis, [(i, i ^ k) for i in range(size)])
    return total


def local(train, query):
    rows = train.shape[0]
    features = train.shape[1] * 16
    partner = swap(train, "xl")
    ex = lax.all_to_all(train.reshape(8, rows // 8, 512), ("zl", "xl"), 0, 0, tiled=True)
    total = factor_terms(ex, input_factor(train))
    total = all_of(total, "co", 2)
    total = all_of(total, "y", 4)
    total = all_of(total, ("xh", "xl"), 4)
    total = all_of(total, "zl", 4)
    inverse = inverses(total, rows * 16 * PROJ)
    other_inverse = swap(inverse, "zh")

    queries = []
    for tag in "qx":
        value = query.T if tag == "q" else swap(value, "xh")
        other = swap(value, "co")
        next_own = ring(value, ("y", "co"), 4)
        next_other = ring(other, ("y", "co"), 4)
        far_own = ring(next_own, ("y", "co"), 4)
        queries.append(
            [
                value,
                other,
                next_own,
                next_other,
                swap(next_own, "co"),
                swap(next_other, "co"),
                far_own,
                swap(far_own, "co"),
            ]
        )
    places = ((0, 0, 0), (0, 0, 1), (0, 1, 0), (0, 1, 1), (0, -1, 1), (0, -1, 0), (2, 0, 0), (2, 0, 1))

    a = jnp.concatenate([train, partner], axis=0)
    b = swap(train, "co")
    ring_axes = ("co",) + Z
    mine, others = [train, partner], []
    for k in range(1, 5):
        a = ring(a, ring_axes, 8)
        mine.append(a)
        if k < 4:
            b = ring(b, ring_axes, 8)
            others += [b, swap(b, "xl")]
    me_row = lax.axis_index(ROW).astype(jnp.int32).reshape(1)
    me_col = lax.axis_index(("co",) + COL).astype(jnp.int32).reshape(1)
    own_places = ((0, 1), (1, 1), (2, 2), (4, 2))
    first = condition_first(me_row, me_col, inverse, *queries, places)
    theirs, own, cond = condition_and_score(
        me_row, me_col, other_inverse, first, *queries, places, others, mine[:4], own_places
    )
    theirs = swap(theirs, "co").astype(F32)
    return (score_own(own, cond, *mine[4:]) + theirs) * (1.0 / math.sqrt(features))


def solution(mesh):
    torus = Mesh(mesh.devices.reshape(2, 4, 2, 2, 4, 2), ROW + COL)
    in_specs = (P(ROW, COL), P(COL, ROW))
    return jax.shard_map(local, mesh=torus, in_specs=in_specs, out_specs=P(ROW, COL), check_vma=False)
```

profile of v0, /device:TPU:1, one launch (start us, length us, event | category | flops | bytes accessed | tf_op | source)
XLA Modules:
  0.0 166.0 jit_solution(16940865662569571837)
XLA Ops:
  0.0 2.0 %collective-permute-start.33 = (bf16[512,512]{1,0:T(8,128)(2,1)}, bf16[512,512]{1,0:T(8,128)(2,1)S(1)}, u32[]{:S(2)}, u32[]{:S(2)}) collective-permute-start(bf16[512,512]{1,0:T(8,128)(2,1)} %refs_26_.1), channel_id=1, source_target_pairs={{0,1},{1,0},{2,3},{3,2},{4,5},{5,4},{6,7},{7,6},{8,9},{9,8},{10,11... | collective-permute-start | bytes 1572872 | tf_op jit(solution)/shard_map/ppermute | solution.py:38
  2.0 5.8 %all-to-all-start = ((bf16[8,64,512]{2,1,0:T(8,128)(2,1)}), bf16[8,64,512]{2,1,0:T(8,128)(2,1)S(1)}, u32[]{:S(2)}, u32[]{:S(2)}) async-start(bf16[8,64,512]{2,1,0:T(8,128)(2,1)} %bitcast.9), calls=%async_computation | async-start | bytes 1048576 | tf_op jit(solution)/shard_map/all_to_all | solution.py:401
  7.8 8.0 %collective-permute-done.33.refs_27_ = bf16[512,512]{1,0:T(8,128)(2,1)S(1)} collective-permute-done((bf16[512,512]{1,0:T(8,128)(2,1)}, bf16[512,512]{1,0:T(8,128)(2,1)S(1)}, u32[]{:S(2)}, u32[]{:S(2)}) %collective-permute-start.33) | collective-permute-done | bytes 524320 | tf_op jit(solution)/shard_map/ppermute | solution.py:38
  15.8 2.3 %pad_maximum_fusion = bf16[1024,512]{1,0:T(8,128)(2,1)} fusion(bf16[512,512]{1,0:T(8,128)(2,1)S(1)} %collective-permute-done.33.refs_27_, bf16[512,512]{1,0:T(8,128)(2,1)} %refs_26_.1), kind=kLoop, calls=%fused_computation | loop fusion | flops 2097152 | bytes 2097152 | tf_op jit(solution)/shard_map/concatenate | solution.py:431
  18.1 7.8 %collective-permute-start.34 = (bf16[1024,512]{1,0:T(8,128)(2,1)}, bf16[1024,512]{1,0:T(8,128)(2,1)}, u32[]{:S(2)}, u32[]{:S(2)}) collective-permute-start(bf16[1024,512]{1,0:T(8,128)(2,1)} %pad_maximum_fusion), channel_id=1, source_target_pairs={{0,2},{2,4},{4,6},{6,8},{8,10},{10,12},{12,14},{14,0},{16,30},{18,... | collective-permute-start | bytes 3145736 | tf_op jit(solution)/shard_map/ppermute | solution.py:34
  26.1 2.8 %collective-permute-start.18 = (bf16[512,512]{1,0:T(8,128)(2,1)S(1)}, bf16[512,512]{1,0:T(8,128)(2,1)S(1)}, u32[]{:S(2)}, u32[]{:S(2)}) collective-permute-start(bf16[512,512]{1,0:T(8,128)(2,1)S(1)} %bitcast.4), channel_id=1, source_target_pairs={{0,128},{128,0},{1,129},{129,1},{2,130},{130,2},{3,131},{131,3},{4... | collective-permute-start | bytes 1572872 | tf_op jit(solution)/shard_map/ppermute | solution.py:38
  29.0 2.7 %collective-permute-start.12 = (bf16[512,512]{1,0:T(8,128)(2,1)S(1)}, bf16[512,512]{1,0:T(8,128)(2,1)S(1)}, u32[]{:S(2)}, u32[]{:S(2)}) collective-permute-start(bf16[512,512]{1,0:T(8,128)(2,1)S(1)} %bitcast.5), channel_id=1, source_target_pairs={{0,32},{32,64},{64,96},{96,0},{16,112},{48,16},{80,48},{112,80},{1... | collective-permute-start | bytes 1572872 | tf_op jit(solution)/shard_map/ppermute | solution.py:34
  32.2 0.5 input_factor.1.input_ref
  32.7 2.3 %factor_terms.1 = f32[2,64,64]{2,1,0:T(8,128)S(1)} custom-call(bf16[8,64,512]{2,1,0:T(8,128)(2,1)S(1)} %all-to-all-done.x_ref, f32[64,64]{1,0:T(8,128)S(1)} %input_factor.1.input_ref), custom_call_target="tpu_custom_call" | custom-call | flops 600000000 | bytes 1048576 | tf_op jit(solution)/shard_map/factor_terms/pallas_call | solution.py:251
  35.1 4.6 %collective-permute-done.18.refs_11_.refs_12_ = bf16[512,512]{1,0:T(8,128)(2,1)S(1)} collective-permute-done((bf16[512,512]{1,0:T(8,128)(2,1)S(1)}, bf16[512,512]{1,0:T(8,128)(2,1)S(1)}, u32[]{:S(2)}, u32[]{:S(2)}) %collective-permute-start.18) | collective-permute-done | bytes 524320 | tf_op jit(solution)/shard_map/ppermute | solution.py:38
  39.7 2.7 %collective-permute-start.20 = (bf16[512,512]{1,0:T(8,128)(2,1)S(1)}, bf16[512,512]{1,0:T(8,128)(2,1)S(1)}, u32[]{:S(2)}, u32[]{:S(2)}) collective-permute-start(bf16[512,512]{1,0:T(8,128)(2,1)S(1)} %collective-permute-done.18.refs_11_.refs_12_), channel_id=1, source_target_pairs={{0,32},{32,64},{64,96},{96,0},{16,112},{48,16},{80,48},{112,80},{1... | collective-permute-start | bytes 1572872 | tf_op jit(solution)/shard_map/ppermute | solution.py:34
  42.5 0.7 collective-permute-start.1
  43.2 6.2 %collective-permute-done.1 = f32[2,64,64]{2,1,0:T(8,128)S(1)} collective-permute-done((f32[2,64,64]{2,1,0:T(8,128)S(1)}, f32[2,64,64]{2,1,0:T(8,128)S(1)}, u32[]{:S(2)}, u32[]{:S(2)}) %collective-permute-start.1) | collective-permute-done | bytes 32800 | tf_op jit(solution)/shard_map/ppermute | solution.py:393
  49.4 2.6 %collective-permute-start.2 = (f32[2,64,64]{2,1,0:T(8,128)S(1)}, f32[2,64,64]{2,1,0:T(8,128)S(1)}, u32[]{:S(2)}, u32[]{:S(2)}) collective-permute-start(f32[2,64,64]{2,1,0:T(8,128)S(1)} %add.53), channel_id=1, source_target_pairs={{0,64},{32,96},{64,0},{96,32},{1,65},{33,97},{65,1},{97,33},{2,66}... | collective-permute-start | bytes 98312 | tf_op jit(solution)/shard_map/ppermute | solution.py:393
  52.1 2.0 %collective-permute-done.2 = f32[2,64,64]{2,1,0:T(8,128)S(1)} collective-permute-done((f32[2,64,64]{2,1,0:T(8,128)S(1)}, f32[2,64,64]{2,1,0:T(8,128)S(1)}, u32[]{:S(2)}, u32[]{:S(2)}) %collective-permute-start.2) | collective-permute-done | bytes 32800 | tf_op jit(solution)/shard_map/ppermute | solution.py:393
  54.1 1.0 collective-permute-start.3
  55.1 3.3 %collective-permute-done.3 = f32[2,64,64]{2,1,0:T(8,128)S(1)} collective-permute-done((f32[2,64,64]{2,1,0:T(8,128)S(1)}, f32[2,64,64]{2,1,0:T(8,128)S(1)}, u32[]{:S(2)}, u32[]{:S(2)}) %collective-permute-start.3) | collective-permute-done | bytes 32800 | tf_op jit(solution)/shard_map/ppermute | solution.py:393
  58.4 1.0 collective-permute-start.16
  59.4 2.4 %collective-permute-start.35 = (bf16[1024,512]{1,0:T(8,128)(2,1)}, bf16[1024,512]{1,0:T(8,128)(2,1)}, u32[]{:S(2)}, u32[]{:S(2)}) collective-permute-start(bf16[1024,512]{1,0:T(8,128)(2,1)} %collective-permute-done.34.refs_28_), channel_id=1, source_target_pairs={{0,2},{2,4},{4,6},{6,8},{8,10},{10,12},{12,14},{14,0},{16,30},{18,... | collective-permute-start | bytes 3145736 | tf_op jit(solution)/shard_map/ppermute | solution.py:34
  61.8 2.0 %collective-permute-start.4 = (f32[2,64,64]{2,1,0:T(8,128)S(1)}, f32[2,64,64]{2,1,0:T(8,128)S(1)}, u32[]{:S(2)}, u32[]{:S(2)}) collective-permute-start(f32[2,64,64]{2,1,0:T(8,128)S(1)} %add_add_fusion.2), channel_id=1, source_target_pairs={{0,1},{1,0},{128,129},{129,128},{2,3},{3,2},{130,131},{131,130},{4... | collective-permute-start | bytes 98312 | tf_op jit(solution)/shard_map/ppermute | solution.py:393
  63.8 1.7 collective-permute-done.4
  65.4 2.5 %collective-permute-start.5 = (f32[2,64,64]{2,1,0:T(8,128)S(1)}, f32[2,64,64]{2,1,0:T(8,128)S(1)}, u32[]{:S(2)}, u32[]{:S(2)}) collective-permute-start(f32[2,64,64]{2,1,0:T(8,128)S(1)} %add_add_fusion.2), channel_id=1, source_target_pairs={{0,128},{1,129},{128,0},{129,1},{2,130},{3,131},{130,2},{131,3},{4... | collective-permute-start | bytes 98312 | tf_op jit(solution)/shard_map/ppermute | solution.py:393
  67.9 2.2 %collective-permute-done.5 = f32[2,64,64]{2,1,0:T(8,128)S(1)} collective-permute-done((f32[2,64,64]{2,1,0:T(8,128)S(1)}, f32[2,64,64]{2,1,0:T(8,128)S(1)}, u32[]{:S(2)}, u32[]{:S(2)}) %collective-permute-start.5) | collective-permute-done | bytes 32800 | tf_op jit(solution)/shard_map/ppermute | solution.py:393
  70.1 2.7 %collective-permute-start.6 = (f32[2,64,64]{2,1,0:T(8,128)S(1)}, f32[2,64,64]{2,1,0:T(8,128)S(1)}, u32[]{:S(2)}, u32[]{:S(2)}) collective-permute-start(f32[2,64,64]{2,1,0:T(8,128)S(1)} %add_add_fusion.2), channel_id=1, source_target_pairs={{0,129},{1,128},{128,1},{129,0},{2,131},{3,130},{130,3},{131,2},{4... | collective-permute-start | bytes 98312 | tf_op jit(solution)/shard_map/ppermute | solution.py:393
  72.8 2.1 %collective-permute-done.6 = f32[2,64,64]{2,1,0:T(8,128)S(1)} collective-permute-done((f32[2,64,64]{2,1,0:T(8,128)S(1)}, f32[2,64,64]{2,1,0:T(8,128)S(1)}, u32[]{:S(2)}, u32[]{:S(2)}) %collective-permute-start.6) | collective-permute-done | bytes 32800 | tf_op jit(solution)/shard_map/ppermute | solution.py:393
  74.9 1.6 collective-permute-start.13
  76.5 3.0 %collective-permute-start.14 = (bf16[512,512]{1,0:T(8,128)(2,1)S(1)}, bf16[512,512]{1,0:T(8,128)(2,1)S(1)}, u32[]{:S(2)}, u32[]{:S(2)}) collective-permute-start(bf16[512,512]{1,0:T(8,128)(2,1)S(1)} %collective-permute-done.12.refs_5_.refs_6_), channel_id=1, source_target_pairs={{0,16},{16,0},{1,17},{17,1},{2,18},{18,2},{3,19},{19,3},{4,20},{20... | collective-permute-start | bytes 1572872 | tf_op jit(solution)/shard_map/ppermute | solution.py:38
  79.4 3.0 %collective-permute-start.27 = (bf16[512,512]{1,0:T(8,128)(2,1)}, bf16[512,512]{1,0:T(8,128)(2,1)S(1)}, u32[]{:S(2)}, u32[]{:S(2)}) collective-permute-start(bf16[512,512]{1,0:T(8,128)(2,1)} %collective-permute-done.26), channel_id=1, source_target_pairs={{0,2},{2,4},{4,6},{6,8},{8,10},{10,12},{12,14},{14,0},{16,30},{18,... | collective-permute-start | bytes 1572872 | tf_op jit(solution)/shard_map/ppermute | solution.py:34
  82.5 2.8 %collective-permute-start.24 = (bf16[512,512]{1,0:T(8,128)(2,1)S(1)}, bf16[512,512]{1,0:T(8,128)(2,1)}, u32[]{:S(2)}, u32[]{:S(2)}) collective-permute-start(bf16[512,512]{1,0:T(8,128)(2,1)S(1)} %collective-permute-done.20.refs_13_.refs_14_), channel_id=1, source_target_pairs={{0,32},{32,64},{64,96},{96,0},{16,112},{48,16},{80,48},{112,80},{1... | collective-permute-start | bytes 1572872 | tf_op jit(solution)/shard_map/ppermute | solution.py:34
  85.4 0.8 copy-done.14
  86.2 0.9 collective-permute-start.8
  87.0 1.9 %collective-permute-done.27.refs_20_ = bf16[512,512]{1,0:T(8,128)(2,1)S(1)} collective-permute-done((bf16[512,512]{1,0:T(8,128)(2,1)}, bf16[512,512]{1,0:T(8,128)(2,1)S(1)}, u32[]{:S(2)}, u32[]{:S(2)}) %collective-permute-start.27) | collective-permute-done | bytes 524320 | tf_op jit(solution)/shard_map/ppermute | solution.py:34
  88.9 3.2 %collective-permute-start.9 = (f32[2,64,64]{2,1,0:T(8,128)S(1)}, f32[2,64,64]{2,1,0:T(8,128)S(1)}, u32[]{:S(2)}, u32[]{:S(2)}) collective-permute-start(f32[2,64,64]{2,1,0:T(8,128)S(1)} %add_add_fusion.1), channel_id=1, source_target_pairs={{0,6},{2,4},{4,2},{6,0},{1,7},{3,5},{5,3},{7,1},{8,14},{10,12},{12... | collective-permute-start | bytes 98312 | tf_op jit(solution)/shard_map/ppermute | solution.py:393
  92.2 1.9 %collective-permute-start.21 = (bf16[512,512]{1,0:T(8,128)(2,1)S(1)}, bf16[512,512]{1,0:T(8,128)(2,1)}, u32[]{:S(2)}, u32[]{:S(2)}) collective-permute-start(bf16[512,512]{1,0:T(8,128)(2,1)S(1)} %collective-permute-done.19.refs_12_.refs_13_), channel_id=1, source_target_pairs={{0,32},{32,64},{64,96},{96,0},{16,112},{48,16},{80,48},{112,80},{1... | collective-permute-start | bytes 1572872 | tf_op jit(solution)/shard_map/ppermute | solution.py:34
  94.0 0.8 copy-done.8
  94.9 3.4 %collective-permute-start.22 = (bf16[512,512]{1,0:T(8,128)(2,1)S(1)}, bf16[512,512]{1,0:T(8,128)(2,1)S(1)}, u32[]{:S(2)}, u32[]{:S(2)}) collective-permute-start(bf16[512,512]{1,0:T(8,128)(2,1)S(1)} %collective-permute-done.20.refs_13_.refs_14_), channel_id=1, source_target_pairs={{0,16},{16,0},{1,17},{17,1},{2,18},{18,2},{3,19},{19,3},{4,20},{20... | collective-permute-start | bytes 1572872 | tf_op jit(solution)/shard_map/ppermute | solution.py:38
  98.3 0.8 copy-done.5
  99.0 0.9 collective-permute-start.29
  100.0 0.8 copy-done.11
  100.8 2.8 %collective-permute-start.36 = (bf16[1024,512]{1,0:T(8,128)(2,1)}, bf16[1024,512]{1,0:T(8,128)(2,1)S(1)}, u32[]{:S(2)}, u32[]{:S(2)}) collective-permute-start(bf16[1024,512]{1,0:T(8,128)(2,1)} %collective-permute-done.35.refs_29_), channel_id=1, source_target_pairs={{0,2},{2,4},{4,6},{6,8},{8,10},{10,12},{12,14},{14,0},{16,30},{18,... | collective-permute-start | bytes 3145736 | tf_op jit(solution)/shard_map/ppermute | solution.py:34
  103.6 1.7 %collective-permute-start.15 = (bf16[512,512]{1,0:T(8,128)(2,1)}, bf16[512,512]{1,0:T(8,128)(2,1)}, u32[]{:S(2)}, u32[]{:S(2)}) collective-permute-start(bf16[512,512]{1,0:T(8,128)(2,1)} %collective-permute-done.13.refs_6_.refs_7_), channel_id=1, source_target_pairs={{0,16},{16,0},{1,17},{17,1},{2,18},{18,2},{3,19},{19,3},{4,20},{20... | collective-permute-start | bytes 1572872 | tf_op jit(solution)/shard_map/ppermute | solution.py:38
  105.3 0.8 copy-done.17
  106.1 1.3 collective-permute-done.29.refs_22_
  107.5 1.8 %collective-permute-start.31 = (bf16[512,512]{1,0:T(8,128)(2,1)}, bf16[512,512]{1,0:T(8,128)(2,1)}, u32[]{:S(2)}, u32[]{:S(2)}) collective-permute-start(bf16[512,512]{1,0:T(8,128)(2,1)} %collective-permute-done.29.refs_22_), channel_id=1, source_target_pairs={{0,2},{2,4},{4,6},{6,8},{8,10},{10,12},{12,14},{14,0},{16,30},{18,... | collective-permute-start | bytes 1572872 | tf_op jit(solution)/shard_map/ppermute | solution.py:34
  109.3 0.8 copy-done.20
  110.1 1.0 collective-permute-start.23
  111.2 1.5 collective-permute-start.30
  112.6 11.7 %collective-permute-done.31.refs_24_ = bf16[512,512]{1,0:T(8,128)(2,1)} collective-permute-done((bf16[512,512]{1,0:T(8,128)(2,1)}, bf16[512,512]{1,0:T(8,128)(2,1)}, u32[]{:S(2)}, u32[]{:S(2)}) %collective-permute-start.31) | collective-permute-done | bytes 524320 | tf_op jit(solution)/shard_map/ppermute | solution.py:34
  124.4 4.5 %inverses.1.refs_2_ = bf16[2,64,64]{2,1,0:T(8,128)(2,1)S(1)} custom-call(f32[2,64,64]{2,1,0:T(8,128)S(1)} %add_add_fusion.refs_0_), custom_call_target="tpu_custom_call" | custom-call | flops 100000000 | bytes 1048576 | tf_op jit(solution)/shard_map/inverses/pallas_call | solution.py:86
  128.9 3.2 %collective-permute-start.10 = (bf16[2,64,64]{2,1,0:T(8,128)(2,1)S(1)}, bf16[2,64,64]{2,1,0:T(8,128)(2,1)S(1)}, u32[]{:S(2)}, u32[]{:S(2)}) collective-permute-start(bf16[2,64,64]{2,1,0:T(8,128)(2,1)S(1)} %inverses.1.refs_2_), channel_id=1, source_target_pairs={{0,8},{8,0},{1,9},{9,1},{2,10},{10,2},{3,11},{11,3},{4,12},{12,4},... | collective-permute-start | bytes 49160 | tf_op jit(solution)/shard_map/ppermute | solution.py:38
  132.1 2.9 %collective-permute-start.37 = (bf16[1024,512]{1,0:T(8,128)(2,1)S(1)}, bf16[1024,512]{1,0:T(8,128)(2,1)S(1)}, u32[]{:S(2)}, u32[]{:S(2)}) collective-permute-start(bf16[1024,512]{1,0:T(8,128)(2,1)S(1)} %collective-permute-done.36.near_ref), channel_id=1, source_target_pairs={{0,2},{2,4},{4,6},{6,8},{8,10},{10,12},{12,14},{14,0},{16,30},{18,... | collective-permute-start | bytes 3145736 | tf_op jit(solution)/shard_map/ppermute | solution.py:34
  135.0 1.0 copy-done.3
  136.0 1.0 copy-done.6
  137.1 1.0 copy-done.9
  138.1 1.0 copy-done.12
  139.1 1.0 copy-done.15
  140.2 1.0 copy-done.18
  141.2 1.0 copy-done.21
  142.3 7.1 %condition_first.1.refs_3_ = bf16[64,64,512]{2,1,0:T(8,128)(2,1)S(1)} custom-call(s32[1]{0:T(128)} %bitcast.refs_0_, s32[1]{0:T(128)} %bitcast.1.refs_1_, bf16[2,64,64]{2,1,0:T(8,128)(2,1)S(1)} %inverses.1.refs_2_, bf16[512,512]{1,0:T(8,128)(2,1)S(1)} %bitcast.7, bf16[512,512]{1,0:T(8,128)(2,1)S(1)} %copy-done.3, ...), custom_call_target="tpu_custom_call" | custom-call | flops 3000000000 | bytes 8388608 | tf_op jit(solution)/shard_map/condition_first/pallas_call | solution.py:182
  149.5 2.0 %copy-done = bf16[64,64,512]{2,1,0:T(8,128)(2,1)} copy-done((bf16[64,64,512]{2,1,0:T(8,128)(2,1)}, bf16[64,64,512]{2,1,0:T(8,128)(2,1)S(1)}, u32[]{:S(2)}) %copy-start) | copy-done | bytes 4194328
  151.5 10.5 %condition_and_score.1 = (bf16[512,512]{1,0:T(8,128)(2,1)S(1)}, f32[512,512]{1,0:T(8,128)S(1)}, bf16[4,8,64,512]{3,2,1,0:T(8,128)(2,1)S(1)}) custom-call(s32[1]{0:T(128)} %bitcast.refs_0_, s32[1]{0:T(128)} %bitcast.1.refs_1_, bf16[2,64,64]{2,1,0:T(8,128)(2,1)S(1)} %collective-permute-done.10.refs_2_, bf16[64,64,512]{2,1,0:T(8,128)(2,1)} %copy-done, ...), custom_call_target="tpu_custom_call" | custom-call | flops 6000000000 | bytes 18874368 | tf_op jit(solution)/shard_map/condition_and_score/pallas_call | solution.py:337
  162.0 1.3 collective-permute-start.38
  163.3 1.2 score_own.1
  164.8 1.1 add_multiply_fusion
  (85 shorter events, 1.3 us)
Async XLA Ops:
  0.0 25.9 %copy-start.27 = (bf16[512,512]{1,0:T(8,128)(2,1)S(1)}, bf16[512,512]{1,0:T(8,128)(2,1)}, u32[]{:S(2)}) copy-start(bf16[512,512]{1,0:T(8,128)(2,1)} %param.3) | copy-start | bytes 1572868
  0.0 15.8 %collective-permute-start.33 = (bf16[512,512]{1,0:T(8,128)(2,1)}, bf16[512,512]{1,0:T(8,128)(2,1)S(1)}, u32[]{:S(2)}, u32[]{:S(2)}) collective-permute-start(bf16[512,512]{1,0:T(8,128)(2,1)} %refs_26_.1), channel_id=1, source_target_pairs={{0,1},{1,0},{2,3},{3,2},{4,5},{5,4},{6,7},{7,6},{8,9},{9,8},{10,11... | collective-permute-start | bytes 1572872 | tf_op jit(solution)/shard_map/ppermute | solution.py:38
  2.0 29.7 %copy-start.1 = (bf16[512,512]{1,0:T(8,128)(2,1)S(1)}, bf16[512,512]{1,0:T(8,128)(2,1)}, u32[]{:S(2)}) copy-start(bf16[512,512]{1,0:T(8,128)(2,1)} %refs_26_.1) | copy-start | bytes 1572868
  2.0 30.7 %all-to-all-start = ((bf16[8,64,512]{2,1,0:T(8,128)(2,1)}), bf16[8,64,512]{2,1,0:T(8,128)(2,1)S(1)}, u32[]{:S(2)}, u32[]{:S(2)}) async-start(bf16[8,64,512]{2,1,0:T(8,128)(2,1)} %bitcast.9), calls=%async_computation | async-start | bytes 1048576 | tf_op jit(solution)/shard_map/all_to_all | solution.py:401
  15.8 2.3 %copy-start.23 = (bf16[512,512]{1,0:T(8,128)(2,1)}, bf16[512,512]{1,0:T(8,128)(2,1)S(1)}, u32[]{:S(2)}) copy-start(bf16[512,512]{1,0:T(8,128)(2,1)S(1)} %collective-permute-done.33.refs_27_) | copy-start | bytes 1572868
  18.1 41.3 %collective-permute-start.34 = (bf16[1024,512]{1,0:T(8,128)(2,1)}, bf16[1024,512]{1,0:T(8,128)(2,1)}, u32[]{:S(2)}, u32[]{:S(2)}) collective-permute-start(bf16[1024,512]{1,0:T(8,128)(2,1)} %pad_maximum_fusion), channel_id=1, source_target_pairs={{0,2},{2,4},{4,6},{6,8},{8,10},{10,12},{12,14},{14,0},{16,30},{18,... | collective-permute-start | bytes 3145736 | tf_op jit(solution)/shard_map/ppermute | solution.py:34
  26.1 13.6 %collective-permute-start.18 = (bf16[512,512]{1,0:T(8,128)(2,1)S(1)}, bf16[512,512]{1,0:T(8,128)(2,1)S(1)}, u32[]{:S(2)}, u32[]{:S(2)}) collective-permute-start(bf16[512,512]{1,0:T(8,128)(2,1)S(1)} %bitcast.4), channel_id=1, source_target_pairs={{0,128},{128,0},{1,129},{129,1},{2,130},{130,2},{3,131},{131,3},{4... | collective-permute-start | bytes 1572872 | tf_op jit(solution)/shard_map/ppermute | solution.py:38
  29.0 10.7 %collective-permute-start.12 = (bf16[512,512]{1,0:T(8,128)(2,1)S(1)}, bf16[512,512]{1,0:T(8,128)(2,1)S(1)}, u32[]{:S(2)}, u32[]{:S(2)}) collective-permute-start(bf16[512,512]{1,0:T(8,128)(2,1)S(1)} %bitcast.5), channel_id=1, source_target_pairs={{0,32},{32,64},{64,96},{96,0},{16,112},{48,16},{80,48},{112,80},{1... | collective-permute-start | bytes 1572872 | tf_op jit(solution)/shard_map/ppermute | solution.py:34
  31.7 10.8 %collective-permute-start.11 = (bf16[512,512]{1,0:T(8,128)(2,1)S(1)}, bf16[512,512]{1,0:T(8,128)(2,1)S(1)}, u32[]{:S(2)}, u32[]{:S(2)}) collective-permute-start(bf16[512,512]{1,0:T(8,128)(2,1)S(1)} %bitcast.6), channel_id=1, source_target_pairs={{0,16},{16,0},{1,17},{17,1},{2,18},{18,2},{3,19},{19,3},{4,20},{20... | collective-permute-start | bytes 1572872 | tf_op jit(solution)/shard_map/ppermute | solution.py:38
  31.7 30.1 %collective-permute-start.26 = (bf16[512,512]{1,0:T(8,128)(2,1)S(1)}, bf16[512,512]{1,0:T(8,128)(2,1)}, u32[]{:S(2)}, u32[]{:S(2)}) collective-permute-start(bf16[512,512]{1,0:T(8,128)(2,1)S(1)} %copy-done.1), channel_id=1, source_target_pairs={{0,16},{16,0},{1,17},{17,1},{2,18},{18,2},{3,19},{19,3},{4,20},{20... | collective-permute-start | bytes 1572872 | tf_op jit(solution)/shard_map/ppermute | solution.py:38
  39.7 2.7 %collective-permute-start = (f32[2,64,64]{2,1,0:T(8,128)S(1)}, f32[2,64,64]{2,1,0:T(8,128)S(1)}, u32[]{:S(2)}, u32[]{:S(2)}) collective-permute-start(f32[2,64,64]{2,1,0:T(8,128)S(1)} %factor_terms.1), channel_id=1, source_target_pairs={{0,16},{16,0},{1,17},{17,1},{2,18},{18,2},{3,19},{19,3},{4,20},{20... | collective-permute-start | bytes 98312 | tf_op jit(solution)/shard_map/ppermute | solution.py:393
  39.7 36.8 %collective-permute-start.20 = (bf16[512,512]{1,0:T(8,128)(2,1)S(1)}, bf16[512,512]{1,0:T(8,128)(2,1)S(1)}, u32[]{:S(2)}, u32[]{:S(2)}) collective-permute-start(bf16[512,512]{1,0:T(8,128)(2,1)S(1)} %collective-permute-done.18.refs_11_.refs_12_), channel_id=1, source_target_pairs={{0,32},{32,64},{64,96},{96,0},{16,112},{48,16},{80,48},{112,80},{1... | collective-permute-start | bytes 1572872 | tf_op jit(solution)/shard_map/ppermute | solution.py:34
  42.4 37.0 %collective-permute-start.19 = (bf16[512,512]{1,0:T(8,128)(2,1)S(1)}, bf16[512,512]{1,0:T(8,128)(2,1)S(1)}, u32[]{:S(2)}, u32[]{:S(2)}) collective-permute-start(bf16[512,512]{1,0:T(8,128)(2,1)S(1)} %collective-permute-done.18.refs_11_.refs_12_), channel_id=1, source_target_pairs={{0,16},{16,0},{1,17},{17,1},{2,18},{18,2},{3,19},{19,3},{4,20},{20... | collective-permute-start | bytes 1572872 | tf_op jit(solution)/shard_map/ppermute | solution.py:38
  42.5 57.5 %copy-start.2 = (bf16[512,512]{1,0:T(8,128)(2,1)}, bf16[512,512]{1,0:T(8,128)(2,1)S(1)}, u32[]{:S(2)}) copy-start(bf16[512,512]{1,0:T(8,128)(2,1)S(1)} %collective-permute-done.11.refs_4_.refs_5_) | copy-start | bytes 1572868
  42.5 7.0 %collective-permute-start.1 = (f32[2,64,64]{2,1,0:T(8,128)S(1)}, f32[2,64,64]{2,1,0:T(8,128)S(1)}, u32[]{:S(2)}, u32[]{:S(2)}) collective-permute-start(f32[2,64,64]{2,1,0:T(8,128)S(1)} %add.53), channel_id=1, source_target_pairs={{0,32},{32,0},{64,96},{96,64},{1,33},{33,1},{65,97},{97,65},{2,34}... | collective-permute-start | bytes 98312 | tf_op jit(solution)/shard_map/ppermute | solution.py:393
  49.4 4.6 %collective-permute-start.2 = (f32[2,64,64]{2,1,0:T(8,128)S(1)}, f32[2,64,64]{2,1,0:T(8,128)S(1)}, u32[]{:S(2)}, u32[]{:S(2)}) collective-permute-start(f32[2,64,64]{2,1,0:T(8,128)S(1)} %add.53), channel_id=1, source_target_pairs={{0,64},{32,96},{64,0},{96,32},{1,65},{33,97},{65,1},{97,33},{2,66}... | collective-permute-start | bytes 98312 | tf_op jit(solution)/shard_map/ppermute | solution.py:393
  54.1 4.3 %collective-permute-start.3 = (f32[2,64,64]{2,1,0:T(8,128)S(1)}, f32[2,64,64]{2,1,0:T(8,128)S(1)}, u32[]{:S(2)}, u32[]{:S(2)}) collective-permute-start(f32[2,64,64]{2,1,0:T(8,128)S(1)} %add.53), channel_id=1, source_target_pairs={{0,96},{32,64},{64,32},{96,0},{1,97},{33,65},{65,33},{97,1},{2,98}... | collective-permute-start | bytes 98312 | tf_op jit(solution)/shard_map/ppermute | solution.py:393
  58.4 24.1 %collective-permute-start.16 = (bf16[512,512]{1,0:T(8,128)(2,1)S(1)}, bf16[512,512]{1,0:T(8,128)(2,1)S(1)}, u32[]{:S(2)}, u32[]{:S(2)}) collective-permute-start(bf16[512,512]{1,0:T(8,128)(2,1)S(1)} %collective-permute-done.12.refs_5_.refs_6_), channel_id=1, source_target_pairs={{0,32},{32,64},{64,96},{96,0},{16,112},{48,16},{80,48},{112,80},{1... | collective-permute-start | bytes 1572872 | tf_op jit(solution)/shard_map/ppermute | solution.py:34
  59.4 41.4 %collective-permute-start.35 = (bf16[1024,512]{1,0:T(8,128)(2,1)}, bf16[1024,512]{1,0:T(8,128)(2,1)}, u32[]{:S(2)}, u32[]{:S(2)}) collective-permute-start(bf16[1024,512]{1,0:T(8,128)(2,1)} %collective-permute-done.34.refs_28_), channel_id=1, source_target_pairs={{0,2},{2,4},{4,6},{6,8},{8,10},{10,12},{12,14},{14,0},{16,30},{18,... | collective-permute-start | bytes 3145736 | tf_op jit(solution)/shard_map/ppermute | solution.py:34
  61.8 3.7 %collective-permute-start.4 = (f32[2,64,64]{2,1,0:T(8,128)S(1)}, f32[2,64,64]{2,1,0:T(8,128)S(1)}, u32[]{:S(2)}, u32[]{:S(2)}) collective-permute-start(f32[2,64,64]{2,1,0:T(8,128)S(1)} %add_add_fusion.2), channel_id=1, source_target_pairs={{0,1},{1,0},{128,129},{129,128},{2,3},{3,2},{130,131},{131,130},{4... | collective-permute-start | bytes 98312 | tf_op jit(solution)/shard_map/ppermute | solution.py:393
  65.4 4.6 %collective-permute-start.5 = (f32[2,64,64]{2,1,0:T(8,128)S(1)}, f32[2,64,64]{2,1,0:T(8,128)S(1)}, u32[]{:S(2)}, u32[]{:S(2)}) collective-permute-start(f32[2,64,64]{2,1,0:T(8,128)S(1)} %add_add_fusion.2), channel_id=1, source_target_pairs={{0,128},{1,129},{128,0},{129,1},{2,130},{3,131},{130,2},{131,3},{4... | collective-permute-start | bytes 98312 | tf_op jit(solution)/shard_map/ppermute | solution.py:393
  70.1 4.8 %collective-permute-start.6 = (f32[2,64,64]{2,1,0:T(8,128)S(1)}, f32[2,64,64]{2,1,0:T(8,128)S(1)}, u32[]{:S(2)}, u32[]{:S(2)}) collective-permute-start(f32[2,64,64]{2,1,0:T(8,128)S(1)} %add_add_fusion.2), channel_id=1, source_target_pairs={{0,129},{1,128},{128,1},{129,0},{2,131},{3,130},{130,3},{131,2},{4... | collective-permute-start | bytes 98312 | tf_op jit(solution)/shard_map/ppermute | solution.py:393
  74.9 10.4 %collective-permute-start.13 = (bf16[512,512]{1,0:T(8,128)(2,1)S(1)}, bf16[512,512]{1,0:T(8,128)(2,1)}, u32[]{:S(2)}, u32[]{:S(2)}) collective-permute-start(bf16[512,512]{1,0:T(8,128)(2,1)S(1)} %collective-permute-done.11.refs_4_.refs_5_), channel_id=1, source_target_pairs={{0,32},{32,64},{64,96},{96,0},{16,112},{48,16},{80,48},{112,80},{1... | collective-permute-start | bytes 1572872 | tf_op jit(solution)/shard_map/ppermute | solution.py:34
  76.5 8.9 %collective-permute-start.14 = (bf16[512,512]{1,0:T(8,128)(2,1)S(1)}, bf16[512,512]{1,0:T(8,128)(2,1)S(1)}, u32[]{:S(2)}, u32[]{:S(2)}) collective-permute-start(bf16[512,512]{1,0:T(8,128)(2,1)S(1)} %collective-permute-done.12.refs_5_.refs_6_), channel_id=1, source_target_pairs={{0,16},{16,0},{1,17},{17,1},{2,18},{18,2},{3,19},{19,3},{4,20},{20... | collective-permute-start | bytes 1572872 | tf_op jit(solution)/shard_map/ppermute | solution.py:38
  79.4 9.5 %collective-permute-start.27 = (bf16[512,512]{1,0:T(8,128)(2,1)}, bf16[512,512]{1,0:T(8,128)(2,1)S(1)}, u32[]{:S(2)}, u32[]{:S(2)}) collective-permute-start(bf16[512,512]{1,0:T(8,128)(2,1)} %collective-permute-done.26), channel_id=1, source_target_pairs={{0,2},{2,4},{4,6},{6,8},{8,10},{10,12},{12,14},{14,0},{16,30},{18,... | collective-permute-start | bytes 1572872 | tf_op jit(solution)/shard_map/ppermute | solution.py:34
  82.5 17.5 %collective-permute-start.24 = (bf16[512,512]{1,0:T(8,128)(2,1)S(1)}, bf16[512,512]{1,0:T(8,128)(2,1)}, u32[]{:S(2)}, u32[]{:S(2)}) collective-permute-start(bf16[512,512]{1,0:T(8,128)(2,1)S(1)} %collective-permute-done.20.refs_13_.refs_14_), channel_id=1, source_target_pairs={{0,32},{32,64},{64,96},{96,0},{16,112},{48,16},{80,48},{112,80},{1... | collective-permute-start | bytes 1572872 | tf_op jit(solution)/shard_map/ppermute | solution.py:34
  85.3 6.9 %collective-permute-start.7 = (f32[2,64,64]{2,1,0:T(8,128)S(1)}, f32[2,64,64]{2,1,0:T(8,128)S(1)}, u32[]{:S(2)}, u32[]{:S(2)}) collective-permute-start(f32[2,64,64]{2,1,0:T(8,128)S(1)} %add_add_fusion.1), channel_id=1, source_target_pairs={{0,2},{2,0},{4,6},{6,4},{1,3},{3,1},{5,7},{7,5},{8,10},{10,8},{12,... | collective-permute-start | bytes 98312 | tf_op jit(solution)/shard_map/ppermute | solution.py:393
  86.2 8.7 %collective-permute-start.8 = (f32[2,64,64]{2,1,0:T(8,128)S(1)}, f32[2,64,64]{2,1,0:T(8,128)S(1)}, u32[]{:S(2)}, u32[]{:S(2)}) collective-permute-start(f32[2,64,64]{2,1,0:T(8,128)S(1)} %add_add_fusion.1), channel_id=1, source_target_pairs={{0,4},{2,6},{4,0},{6,2},{1,5},{3,7},{5,1},{7,3},{8,12},{10,14},{12... | collective-permute-start | bytes 98312 | tf_op jit(solution)/shard_map/ppermute | solution.py:393
  88.9 20.4 %copy-start.25 = (bf16[512,512]{1,0:T(8,128)(2,1)}, bf16[512,512]{1,0:T(8,128)(2,1)S(1)}, u32[]{:S(2)}) copy-start(bf16[512,512]{1,0:T(8,128)(2,1)S(1)} %collective-permute-done.27.refs_20_) | copy-start | bytes 1572868
  88.9 10.1 %collective-permute-start.9 = (f32[2,64,64]{2,1,0:T(8,128)S(1)}, f32[2,64,64]{2,1,0:T(8,128)S(1)}, u32[]{:S(2)}, u32[]{:S(2)}) collective-permute-start(f32[2,64,64]{2,1,0:T(8,128)S(1)} %add_add_fusion.1), channel_id=1, source_target_pairs={{0,6},{2,4},{4,2},{6,0},{1,7},{3,5},{5,3},{7,1},{8,14},{10,12},{12... | collective-permute-start | bytes 98312 | tf_op jit(solution)/shard_map/ppermute | solution.py:393
  92.2 11.5 %collective-permute-start.21 = (bf16[512,512]{1,0:T(8,128)(2,1)S(1)}, bf16[512,512]{1,0:T(8,128)(2,1)}, u32[]{:S(2)}, u32[]{:S(2)}) collective-permute-start(bf16[512,512]{1,0:T(8,128)(2,1)S(1)} %collective-permute-done.19.refs_12_.refs_13_), channel_id=1, source_target_pairs={{0,32},{32,64},{64,96},{96,0},{16,112},{48,16},{80,48},{112,80},{1... | collective-permute-start | bytes 1572872 | tf_op jit(solution)/shard_map/ppermute | solution.py:34
  94.0 0.8 copy-start.8
  94.9 10.5 %collective-permute-start.22 = (bf16[512,512]{1,0:T(8,128)(2,1)S(1)}, bf16[512,512]{1,0:T(8,128)(2,1)S(1)}, u32[]{:S(2)}, u32[]{:S(2)}) collective-permute-start(bf16[512,512]{1,0:T(8,128)(2,1)S(1)} %collective-permute-done.20.refs_13_.refs_14_), channel_id=1, source_target_pairs={{0,16},{16,0},{1,17},{17,1},{2,18},{18,2},{3,19},{19,3},{4,20},{20... | collective-permute-start | bytes 1572872 | tf_op jit(solution)/shard_map/ppermute | solution.py:38
  99.0 8.4 %collective-permute-start.29 = (bf16[512,512]{1,0:T(8,128)(2,1)S(1)}, bf16[512,512]{1,0:T(8,128)(2,1)}, u32[]{:S(2)}, u32[]{:S(2)}) collective-permute-start(bf16[512,512]{1,0:T(8,128)(2,1)S(1)} %collective-permute-done.27.refs_20_), channel_id=1, source_target_pairs={{0,2},{2,4},{4,6},{6,8},{8,10},{10,12},{12,14},{14,0},{16,30},{18,... | collective-permute-start | bytes 1572872 | tf_op jit(solution)/shard_map/ppermute | solution.py:34
  99.9 9.3 %collective-permute-start.17 = (bf16[512,512]{1,0:T(8,128)(2,1)S(1)}, bf16[512,512]{1,0:T(8,128)(2,1)S(1)}, u32[]{:S(2)}, u32[]{:S(2)}) collective-permute-start(bf16[512,512]{1,0:T(8,128)(2,1)S(1)} %collective-permute-done.16.refs_9_.refs_10_), channel_id=1, source_target_pairs={{0,16},{16,0},{1,17},{17,1},{2,18},{18,2},{3,19},{19,3},{4,20},{20... | collective-permute-start | bytes 1572872 | tf_op jit(solution)/shard_map/ppermute | solution.py:38
  100.0 0.8 copy-start.11
  100.8 31.3 %collective-permute-start.36 = (bf16[1024,512]{1,0:T(8,128)(2,1)}, bf16[1024,512]{1,0:T(8,128)(2,1)S(1)}, u32[]{:S(2)}, u32[]{:S(2)}) collective-permute-start(bf16[1024,512]{1,0:T(8,128)(2,1)} %collective-permute-done.35.refs_29_), channel_id=1, source_target_pairs={{0,2},{2,4},{4,6},{6,8},{8,10},{10,12},{12,14},{14,0},{16,30},{18,... | collective-permute-start | bytes 3145736 | tf_op jit(solution)/shard_map/ppermute | solution.py:34
  103.6 7.5 %collective-permute-start.15 = (bf16[512,512]{1,0:T(8,128)(2,1)}, bf16[512,512]{1,0:T(8,128)(2,1)}, u32[]{:S(2)}, u32[]{:S(2)}) collective-permute-start(bf16[512,512]{1,0:T(8,128)(2,1)} %collective-permute-done.13.refs_6_.refs_7_), channel_id=1, source_target_pairs={{0,16},{16,0},{1,17},{17,1},{2,18},{18,2},{3,19},{19,3},{4,20},{20... | collective-permute-start | bytes 1572872 | tf_op jit(solution)/shard_map/ppermute | solution.py:38
  106.1 5.0 %collective-permute-start.25 = (bf16[512,512]{1,0:T(8,128)(2,1)}, bf16[512,512]{1,0:T(8,128)(2,1)}, u32[]{:S(2)}, u32[]{:S(2)}) collective-permute-start(bf16[512,512]{1,0:T(8,128)(2,1)} %collective-permute-done.24.refs_17_.refs_18_), channel_id=1, source_target_pairs={{0,16},{16,0},{1,17},{17,1},{2,18},{18,2},{3,19},{19,3},{4,20},{20... | collective-permute-start | bytes 1572872 | tf_op jit(solution)/shard_map/ppermute | solution.py:38
  107.5 16.9 %collective-permute-start.31 = (bf16[512,512]{1,0:T(8,128)(2,1)}, bf16[512,512]{1,0:T(8,128)(2,1)}, u32[]{:S(2)}, u32[]{:S(2)}) collective-permute-start(bf16[512,512]{1,0:T(8,128)(2,1)} %collective-permute-done.29.refs_22_), channel_id=1, source_target_pairs={{0,2},{2,4},{4,6},{6,8},{8,10},{10,12},{12,14},{14,0},{16,30},{18,... | collective-permute-start | bytes 1572872 | tf_op jit(solution)/shard_map/ppermute | solution.py:34
  110.1 18.8 %collective-permute-start.23 = (bf16[512,512]{1,0:T(8,128)(2,1)}, bf16[512,512]{1,0:T(8,128)(2,1)}, u32[]{:S(2)}, u32[]{:S(2)}) collective-permute-start(bf16[512,512]{1,0:T(8,128)(2,1)} %collective-permute-done.21.refs_14_.refs_15_), channel_id=1, source_target_pairs={{0,16},{16,0},{1,17},{17,1},{2,18},{18,2},{3,19},{19,3},{4,20},{20... | collective-permute-start | bytes 1572872 | tf_op jit(solution)/shard_map/ppermute | solution.py:38
  111.1 40.3 %collective-permute-start.28 = (bf16[512,512]{1,0:T(8,128)(2,1)}, bf16[512,512]{1,0:T(8,128)(2,1)}, u32[]{:S(2)}, u32[]{:S(2)}) collective-permute-start(bf16[512,512]{1,0:T(8,128)(2,1)} %copy-done.25), channel_id=1, source_target_pairs={{0,1},{1,0},{2,3},{3,2},{4,5},{5,4},{6,7},{7,6},{8,9},{9,8},{10,11... | collective-permute-start | bytes 1572872 | tf_op jit(solution)/shard_map/ppermute | solution.py:38
  111.2 40.3 %collective-permute-start.30 = (bf16[512,512]{1,0:T(8,128)(2,1)}, bf16[512,512]{1,0:T(8,128)(2,1)}, u32[]{:S(2)}, u32[]{:S(2)}) collective-permute-start(bf16[512,512]{1,0:T(8,128)(2,1)} %collective-permute-done.29.refs_22_), channel_id=1, source_target_pairs={{0,1},{1,0},{2,3},{3,2},{4,5},{5,4},{6,7},{7,6},{8,9},{9,8},{10,11... | collective-permute-start | bytes 1572872 | tf_op jit(solution)/shard_map/ppermute | solution.py:38
  124.3 27.1 %collective-permute-start.32 = (bf16[512,512]{1,0:T(8,128)(2,1)}, bf16[512,512]{1,0:T(8,128)(2,1)}, u32[]{:S(2)}, u32[]{:S(2)}) collective-permute-start(bf16[512,512]{1,0:T(8,128)(2,1)} %collective-permute-done.31.refs_24_), channel_id=1, source_target_pairs={{0,1},{1,0},{2,3},{3,2},{4,5},{5,4},{6,7},{7,6},{8,9},{9,8},{10,11... | collective-permute-start | bytes 1572872 | tf_op jit(solution)/shard_map/ppermute | solution.py:38
  128.9 22.6 %collective-permute-start.10 = (bf16[2,64,64]{2,1,0:T(8,128)(2,1)S(1)}, bf16[2,64,64]{2,1,0:T(8,128)(2,1)S(1)}, u32[]{:S(2)}, u32[]{:S(2)}) collective-permute-start(bf16[2,64,64]{2,1,0:T(8,128)(2,1)S(1)} %inverses.1.refs_2_), channel_id=1, source_target_pairs={{0,8},{8,0},{1,9},{9,1},{2,10},{10,2},{3,11},{11,3},{4,12},{12,4},... | collective-permute-start | bytes 49160 | tf_op jit(solution)/shard_map/ppermute | solution.py:38
  132.1 31.2 %collective-permute-start.37 = (bf16[1024,512]{1,0:T(8,128)(2,1)S(1)}, bf16[1024,512]{1,0:T(8,128)(2,1)S(1)}, u32[]{:S(2)}, u32[]{:S(2)}) collective-permute-start(bf16[1024,512]{1,0:T(8,128)(2,1)S(1)} %collective-permute-done.36.near_ref), channel_id=1, source_target_pairs={{0,2},{2,4},{4,6},{6,8},{8,10},{10,12},{12,14},{14,0},{16,30},{18,... | collective-permute-start | bytes 3145736 | tf_op jit(solution)/shard_map/ppermute | solution.py:34
  135.0 1.0 copy-start.3
  136.0 1.0 copy-start.6
  137.1 1.0 copy-start.9
  138.1 1.0 copy-start.12
  139.1 1.0 copy-start.15
  140.2 1.0 copy-start.18
  141.2 1.0 copy-start.21
  142.3 9.2 %copy-start.4 = (bf16[512,512]{1,0:T(8,128)(2,1)S(1)}, bf16[512,512]{1,0:T(8,128)(2,1)}, u32[]{:S(2)}) copy-start(bf16[512,512]{1,0:T(8,128)(2,1)} %copy-done.2) | copy-start | bytes 1572868
  142.3 9.2 %copy-start.7 = (bf16[512,512]{1,0:T(8,128)(2,1)S(1)}, bf16[512,512]{1,0:T(8,128)(2,1)}, u32[]{:S(2)}) copy-start(bf16[512,512]{1,0:T(8,128)(2,1)} %copy-done.5) | copy-start | bytes 1572868
  142.3 9.2 %copy-start.10 = (bf16[512,512]{1,0:T(8,128)(2,1)S(1)}, bf16[512,512]{1,0:T(8,128)(2,1)}, u32[]{:S(2)}) copy-start(bf16[512,512]{1,0:T(8,128)(2,1)} %copy-done.8) | copy-start | bytes 1572868
  142.3 9.2 %copy-start.13 = (bf16[512,512]{1,0:T(8,128)(2,1)S(1)}, bf16[512,512]{1,0:T(8,128)(2,1)}, u32[]{:S(2)}) copy-start(bf16[512,512]{1,0:T(8,128)(2,1)} %copy-done.11) | copy-start | bytes 1572868
  142.3 9.2 %copy-start.16 = (bf16[512,512]{1,0:T(8,128)(2,1)S(1)}, bf16[512,512]{1,0:T(8,128)(2,1)}, u32[]{:S(2)}) copy-start(bf16[512,512]{1,0:T(8,128)(2,1)} %copy-done.14) | copy-start | bytes 1572868
  142.3 9.2 %copy-start.19 = (bf16[512,512]{1,0:T(8,128)(2,1)S(1)}, bf16[512,512]{1,0:T(8,128)(2,1)}, u32[]{:S(2)}) copy-start(bf16[512,512]{1,0:T(8,128)(2,1)} %copy-done.17) | copy-start | bytes 1572868
  142.3 9.2 %copy-start.22 = (bf16[512,512]{1,0:T(8,128)(2,1)S(1)}, bf16[512,512]{1,0:T(8,128)(2,1)}, u32[]{:S(2)}) copy-start(bf16[512,512]{1,0:T(8,128)(2,1)} %copy-done.20) | copy-start | bytes 1572868
  142.3 9.2 %copy-start.24 = (bf16[512,512]{1,0:T(8,128)(2,1)S(1)}, bf16[512,512]{1,0:T(8,128)(2,1)}, u32[]{:S(2)}) copy-start(bf16[512,512]{1,0:T(8,128)(2,1)} %copy-done.23) | copy-start | bytes 1572868
  142.3 9.2 %copy-start.26 = (bf16[512,512]{1,0:T(8,128)(2,1)S(1)}, bf16[512,512]{1,0:T(8,128)(2,1)}, u32[]{:S(2)}) copy-start(bf16[512,512]{1,0:T(8,128)(2,1)} %copy-done.25) | copy-start | bytes 1572868
  149.4 2.0 %copy-start = (bf16[64,64,512]{2,1,0:T(8,128)(2,1)}, bf16[64,64,512]{2,1,0:T(8,128)(2,1)S(1)}, u32[]{:S(2)}) copy-start(bf16[64,64,512]{2,1,0:T(8,128)(2,1)S(1)} %condition_first.1.refs_3_) | copy-start | bytes 12582916
  162.0 2.8 %collective-permute-start.38 = (bf16[512,512]{1,0:T(8,128)(2,1)S(1)}, bf16[512,512]{1,0:T(8,128)(2,1)S(1)}, u32[]{:S(2)}, u32[]{:S(2)}) collective-permute-start(bf16[512,512]{1,0:T(8,128)(2,1)S(1)} %get-tuple-element.10), channel_id=1, source_target_pairs={{0,16},{16,0},{1,17},{17,1},{2,18},{18,2},{3,19},{19,3},{4,20},{20... | collective-permute-start | bytes 1572872 | tf_op jit(solution)/shard_map/ppermute | solution.py:38
  (4 other events, 3.2 us)
where the time goes:
time: 166 us
  starting transfers between devices  76.3 us (46%)
  waiting for transfers between devices  45.3 us (27%)
  Pallas kernels  26.2 us (16%)
  local copies, waits for them, and re-layouts  14.3 us (9%)
  other arithmetic  3.47 us (2%)
    ppermute x13, starting transfers between devices, ring(): return lax.ppermute(value, axes, pairs)  34.4 us
    ppermute x16, starting transfers between devices, swap(): return lax.ppermute(value, axis, SWAP)  20.4 us
    ppermute x10, waiting for transfers between devices, all_of(): total = total + lax.ppermute(value, axis, [(i, i ^ k) for i in range(size)])  17.4 us
    ppermute x10, starting transfers between devices, all_of(): total = total + lax.ppermute(value, axis, [(i, i ^ k) for i in range(size)])  15.8 us
    ppermute x13, waiting for transfers between devices, ring(): return lax.ppermute(value, axes, pairs)  14.9 us
    unnamed x57, local copies, waits for them, and re-layouts  14.3 us
    ppermute x16, waiting for transfers between devices, swap(): return lax.ppermute(value, axis, SWAP)  12.9 us
    pallas_call x1, Pallas kernels, condition_and_score(): pl.pallas_call(lambda *refs: main_kernel(places, own_places, *refs), out_...  10.5 us
  transfers between devices with their start and end apart: 40, of which 12 were waited for; matrix products, arithmetic and copies ran while one was open for 2% of the time, Pallas kernels for 16%

commit v1 on v0

--- a/solution.py
+++ b/solution.py
@@ -158,23 +158,16 @@
 
 def first_kernel(places, me_row_ref, me_col_ref, inverse_ref, *refs):
     near, far = refs[:8], refs[8:16]
-    out_ref, query_buf, half_ref, cond_ref, wide_in_ref, wide_out_ref, query_sem, out_sem = refs[16:]
+    out_ref, query_buf, half_ref, wide_in_ref, wide_out_ref, query_sem = refs[16:]
     me = me_row_ref[0]
     layer = (me_col_ref[0] // 8) % 2
     copies = fetch_queries(near, far, me // 8 == layer, query_buf, query_sem)
     expand(inverse_ref, wide_in_ref, wide_out_ref)
 
-    def out_copy(k, start):
-        rows = pl.ds(start, 16)
-        return pltpu.make_async_copy(cond_ref.at[:, rows, :], out_ref.at[:, rows, :], out_sem.at[k])
-
     def store(k, start, value):
-        cond_ref[:, pl.ds(start, 16), :] = value
-        out_copy(k, start).start()
+        out_ref[:, pl.ds(start, 16), :] = value
 
     condition_layer(places, me, copies, query_buf, half_ref, wide_in_ref, wide_out_ref, store)
-    for k in range(4):
-        out_copy(k, 16 * k).wait()
 
 
 def condition_first(me_row, me_col, inverse, near, far, places):
@@ -183,17 +176,15 @@
         lambda *refs: first_kernel(places, *refs),
         out_shape=jax.ShapeDtypeStruct((PROJ, PROJ, width), BF16),
         in_specs=[SMEM, SMEM, VMEM] + [ANY] * 16,
-        out_specs=HBM,
+        out_specs=VMEM,
         scratch_shapes=[
             pltpu.VMEM((8, 512, width), BF16),
             pltpu.VMEM((8, 512, width), BF16),
-            pltpu.VMEM((PROJ, PROJ, width), BF16),
             pltpu.VMEM((256, 256), BF16),
             pltpu.VMEM((512, 512), BF16),
             pltpu.SemaphoreType.DMA((8,)),
-            pltpu.SemaphoreType.DMA((4,)),
         ],
-        compiler_params=pltpu.CompilerParams(vmem_limit_bytes=20 << 20),
+        compiler_params=pltpu.CompilerParams(vmem_limit_bytes=18 << 20),
         cost_estimate=pl.CostEstimate(flops=3 * 10**9, bytes_accessed=8 << 20, transcendentals=0),
         name="condition_first",
     )(me_row, me_col, inverse, *near, *far)
@@ -341,7 +332,7 @@
             jax.ShapeDtypeStruct((512, width), F32),
             jax.ShapeDtypeStruct((4, 8, PROJ, width), BF16),
         ),
-        in_specs=[SMEM, SMEM, VMEM, HBM] + [ANY] * (16 + len(theirs) + len(own)),
+        in_specs=[SMEM, SMEM, VMEM, ANY] + [ANY] * (16 + len(theirs) + len(own)),
         out_specs=(VMEM, VMEM, HBM),
         scratch_shapes=[
             pltpu.VMEM((8, 512, width), BF16),
@@ -358,7 +349,7 @@
             pltpu.SemaphoreType.DMA((4,)),
             pltpu.SemaphoreType.DMA((1,)),
         ],
-        compiler_params=pltpu.CompilerParams(vmem_limit_bytes=34 << 20),
+        compiler_params=pltpu.CompilerParams(vmem_limit_bytes=28 << 20),
         cost_estimate=pl.CostEstimate(flops=6 * 10**9, bytes_accessed=18 << 20, transcendentals=0),
         name="condition_and_score",
     )(me_row, me_col, inverse, first, *near, *far, *theirs, *own)

time: 166 us -> 164 us (0.988)
  local copies, waits for them, and re-layouts: 14.3 us -> 12.3 us
    unnamed x57 -> x55, local copies, waits for them, and re-layouts: 14.3 us -> 12.3 us
where the time goes in v1:
time: 164 us; the launch traced here: 163 us
  starting transfers between devices  76.4 us (47%)
  waiting for transfers between devices  45.3 us (28%)
  Pallas kernels  25.4 us (15%)
  local copies, waits for them, and re-layouts  12.3 us (8%)
  other arithmetic  3.47 us (2%)
    ppermute x13, starting transfers between devices, ring(): return lax.ppermute(value, axes, pairs)  34.4 us
    ppermute x16, starting transfers between devices, swap(): return lax.ppermute(value, axis, SWAP)  20.4 us
    ppermute x10, waiting for transfers between devices, all_of(): total = total + lax.ppermute(value, axis, [(i, i ^ k) for i in range(size)])  17.4 us
    ppermute x10, starting transfers between devices, all_of(): total = total + lax.ppermute(value, axis, [(i, i ^ k) for i in range(size)])  15.8 us
    ppermute x13, waiting for transfers between devices, ring(): return lax.ppermute(value, axes, pairs)  14.9 us
    ppermute x16, waiting for transfers between devices, swap(): return lax.ppermute(value, axis, SWAP)  12.9 us
    unnamed x55, local copies, waits for them, and re-layouts  12.3 us
    pallas_call x1, Pallas kernels, condition_and_score(): pl.pallas_call(lambda *refs: main_kernel(places, own_places, *refs), out_...  10.7 us
  transfers between devices with their start and end apart: 40, of which 12 were waited for; matrix products, arithmetic and copies ran while one was open for 2% of the time, Pallas kernels for 16%

profile of v1, /device:TPU:1, one launch (start us, length us, event | category | flops | bytes accessed | tf_op | source)
XLA Modules:
  0.0 163.2 jit_solution(9917136708204542425)
XLA Ops:
  0.0 2.0 %collective-permute-start.33 = (bf16[512,512]{1,0:T(8,128)(2,1)}, bf16[512,512]{1,0:T(8,128)(2,1)S(1)}, u32[]{:S(2)}, u32[]{:S(2)}) collective-permute-start(bf16[512,512]{1,0:T(8,128)(2,1)} %refs_26_.1), channel_id=1, source_target_pairs={{0,1},{1,0},{2,3},{3,2},{4,5},{5,4},{6,7},{7,6},{8,9},{9,8},{10,11... | collective-permute-start | bytes 1572872 | tf_op jit(solution)/shard_map/ppermute | solution.py:38
  2.0 5.8 %all-to-all-start = ((bf16[8,64,512]{2,1,0:T(8,128)(2,1)}), bf16[8,64,512]{2,1,0:T(8,128)(2,1)S(1)}, u32[]{:S(2)}, u32[]{:S(2)}) async-start(bf16[8,64,512]{2,1,0:T(8,128)(2,1)} %bitcast.9), calls=%async_computation | async-start | bytes 1048576 | tf_op jit(solution)/shard_map/all_to_all | solution.py:392
  7.8 8.0 %collective-permute-done.33.refs_27_ = bf16[512,512]{1,0:T(8,128)(2,1)S(1)} collective-permute-done((bf16[512,512]{1,0:T(8,128)(2,1)}, bf16[512,512]{1,0:T(8,128)(2,1)S(1)}, u32[]{:S(2)}, u32[]{:S(2)}) %collective-permute-start.33) | collective-permute-done | bytes 524320 | tf_op jit(solution)/shard_map/ppermute | solution.py:38
  15.8 2.3 %pad_maximum_fusion = bf16[1024,512]{1,0:T(8,128)(2,1)} fusion(bf16[512,512]{1,0:T(8,128)(2,1)S(1)} %collective-permute-done.33.refs_27_, bf16[512,512]{1,0:T(8,128)(2,1)} %refs_26_.1), kind=kLoop, calls=%fused_computation | loop fusion | flops 2097152 | bytes 2097152 | tf_op jit(solution)/shard_map/concatenate | solution.py:422
  18.1 7.8 %collective-permute-start.34 = (bf16[1024,512]{1,0:T(8,128)(2,1)}, bf16[1024,512]{1,0:T(8,128)(2,1)}, u32[]{:S(2)}, u32[]{:S(2)}) collective-permute-start(bf16[1024,512]{1,0:T(8,128)(2,1)} %pad_maximum_fusion), channel_id=1, source_target_pairs={{0,2},{2,4},{4,6},{6,8},{8,10},{10,12},{12,14},{14,0},{16,30},{18,... | collective-permute-start | bytes 3145736 | tf_op jit(solution)/shard_map/ppermute | solution.py:34
  26.1 2.8 %collective-permute-start.18 = (bf16[512,512]{1,0:T(8,128)(2,1)S(1)}, bf16[512,512]{1,0:T(8,128)(2,1)S(1)}, u32[]{:S(2)}, u32[]{:S(2)}) collective-permute-start(bf16[512,512]{1,0:T(8,128)(2,1)S(1)} %bitcast.4), channel_id=1, source_target_pairs={{0,128},{128,0},{1,129},{129,1},{2,130},{130,2},{3,131},{131,3},{4... | collective-permute-start | bytes 1572872 | tf_op jit(solution)/shard_map/ppermute | solution.py:38
  29.0 2.7 %collective-permute-start.12 = (bf16[512,512]{1,0:T(8,128)(2,1)S(1)}, bf16[512,512]{1,0:T(8,128)(2,1)S(1)}, u32[]{:S(2)}, u32[]{:S(2)}) collective-permute-start(bf16[512,512]{1,0:T(8,128)(2,1)S(1)} %bitcast.5), channel_id=1, source_target_pairs={{0,32},{32,64},{64,96},{96,0},{16,112},{48,16},{80,48},{112,80},{1... | collective-permute-start | bytes 1572872 | tf_op jit(solution)/shard_map/ppermute | solution.py:34
  31.7 0.5 collective-permute-start.26
  32.2 0.5 input_factor.1.input_ref
  32.7 2.3 %factor_terms.1 = f32[2,64,64]{2,1,0:T(8,128)S(1)} custom-call(bf16[8,64,512]{2,1,0:T(8,128)(2,1)S(1)} %all-to-all-done.x_ref, f32[64,64]{1,0:T(8,128)S(1)} %input_factor.1.input_ref), custom_call_target="tpu_custom_call" | custom-call | flops 600000000 | bytes 1048576 | tf_op jit(solution)/shard_map/factor_terms/pallas_call | solution.py:242
  35.1 4.6 %collective-permute-done.18.refs_11_.refs_12_ = bf16[512,512]{1,0:T(8,128)(2,1)S(1)} collective-permute-done((bf16[512,512]{1,0:T(8,128)(2,1)S(1)}, bf16[512,512]{1,0:T(8,128)(2,1)S(1)}, u32[]{:S(2)}, u32[]{:S(2)}) %collective-permute-start.18) | collective-permute-done | bytes 524320 | tf_op jit(solution)/shard_map/ppermute | solution.py:38
  39.7 2.7 %collective-permute-start.20 = (bf16[512,512]{1,0:T(8,128)(2,1)S(1)}, bf16[512,512]{1,0:T(8,128)(2,1)S(1)}, u32[]{:S(2)}, u32[]{:S(2)}) collective-permute-start(bf16[512,512]{1,0:T(8,128)(2,1)S(1)} %collective-permute-done.18.refs_11_.refs_12_), channel_id=1, source_target_pairs={{0,32},{32,64},{64,96},{96,0},{16,112},{48,16},{80,48},{112,80},{1... | collective-permute-start | bytes 1572872 | tf_op jit(solution)/shard_map/ppermute | solution.py:34
  42.5 0.7 collective-permute-start.1
  43.2 6.2 %collective-permute-done.1 = f32[2,64,64]{2,1,0:T(8,128)S(1)} collective-permute-done((f32[2,64,64]{2,1,0:T(8,128)S(1)}, f32[2,64,64]{2,1,0:T(8,128)S(1)}, u32[]{:S(2)}, u32[]{:S(2)}) %collective-permute-start.1) | collective-permute-done | bytes 32800 | tf_op jit(solution)/shard_map/ppermute | solution.py:384
  49.4 2.6 %collective-permute-start.2 = (f32[2,64,64]{2,1,0:T(8,128)S(1)}, f32[2,64,64]{2,1,0:T(8,128)S(1)}, u32[]{:S(2)}, u32[]{:S(2)}) collective-permute-start(f32[2,64,64]{2,1,0:T(8,128)S(1)} %add.53), channel_id=1, source_target_pairs={{0,64},{32,96},{64,0},{96,32},{1,65},{33,97},{65,1},{97,33},{2,66}... | collective-permute-start | bytes 98312 | tf_op jit(solution)/shard_map/ppermute | solution.py:384
  52.1 2.0 %collective-permute-done.2 = f32[2,64,64]{2,1,0:T(8,128)S(1)} collective-permute-done((f32[2,64,64]{2,1,0:T(8,128)S(1)}, f32[2,64,64]{2,1,0:T(8,128)S(1)}, u32[]{:S(2)}, u32[]{:S(2)}) %collective-permute-start.2) | collective-permute-done | bytes 32800 | tf_op jit(solution)/shard_map/ppermute | solution.py:384
  54.1 1.0 collective-permute-start.3
  55.1 3.3 %collective-permute-done.3 = f32[2,64,64]{2,1,0:T(8,128)S(1)} collective-permute-done((f32[2,64,64]{2,1,0:T(8,128)S(1)}, f32[2,64,64]{2,1,0:T(8,128)S(1)}, u32[]{:S(2)}, u32[]{:S(2)}) %collective-permute-start.3) | collective-permute-done | bytes 32800 | tf_op jit(solution)/shard_map/ppermute | solution.py:384
  58.4 1.0 collective-permute-start.16
  59.4 2.4 %collective-permute-start.35 = (bf16[1024,512]{1,0:T(8,128)(2,1)}, bf16[1024,512]{1,0:T(8,128)(2,1)}, u32[]{:S(2)}, u32[]{:S(2)}) collective-permute-start(bf16[1024,512]{1,0:T(8,128)(2,1)} %collective-permute-done.34.refs_28_), channel_id=1, source_target_pairs={{0,2},{2,4},{4,6},{6,8},{8,10},{10,12},{12,14},{14,0},{16,30},{18,... | collective-permute-start | bytes 3145736 | tf_op jit(solution)/shard_map/ppermute | solution.py:34
  61.8 2.0 %collective-permute-start.4 = (f32[2,64,64]{2,1,0:T(8,128)S(1)}, f32[2,64,64]{2,1,0:T(8,128)S(1)}, u32[]{:S(2)}, u32[]{:S(2)}) collective-permute-start(f32[2,64,64]{2,1,0:T(8,128)S(1)} %add_add_fusion.2), channel_id=1, source_target_pairs={{0,1},{1,0},{128,129},{129,128},{2,3},{3,2},{130,131},{131,130},{4... | collective-permute-start | bytes 98312 | tf_op jit(solution)/shard_map/ppermute | solution.py:384
  63.8 1.7 %collective-permute-done.4 = f32[2,64,64]{2,1,0:T(8,128)S(1)} collective-permute-done((f32[2,64,64]{2,1,0:T(8,128)S(1)}, f32[2,64,64]{2,1,0:T(8,128)S(1)}, u32[]{:S(2)}, u32[]{:S(2)}) %collective-permute-start.4) | collective-permute-done | bytes 32800 | tf_op jit(solution)/shard_map/ppermute | solution.py:384
  65.4 2.5 %collective-permute-start.5 = (f32[2,64,64]{2,1,0:T(8,128)S(1)}, f32[2,64,64]{2,1,0:T(8,128)S(1)}, u32[]{:S(2)}, u32[]{:S(2)}) collective-permute-start(f32[2,64,64]{2,1,0:T(8,128)S(1)} %add_add_fusion.2), channel_id=1, source_target_pairs={{0,128},{1,129},{128,0},{129,1},{2,130},{3,131},{130,2},{131,3},{4... | collective-permute-start | bytes 98312 | tf_op jit(solution)/shard_map/ppermute | solution.py:384
  67.9 2.2 %collective-permute-done.5 = f32[2,64,64]{2,1,0:T(8,128)S(1)} collective-permute-done((f32[2,64,64]{2,1,0:T(8,128)S(1)}, f32[2,64,64]{2,1,0:T(8,128)S(1)}, u32[]{:S(2)}, u32[]{:S(2)}) %collective-permute-start.5) | collective-permute-done | bytes 32800 | tf_op jit(solution)/shard_map/ppermute | solution.py:384
  70.1 2.7 %collective-permute-start.6 = (f32[2,64,64]{2,1,0:T(8,128)S(1)}, f32[2,64,64]{2,1,0:T(8,128)S(1)}, u32[]{:S(2)}, u32[]{:S(2)}) collective-permute-start(f32[2,64,64]{2,1,0:T(8,128)S(1)} %add_add_fusion.2), channel_id=1, source_target_pairs={{0,129},{1,128},{128,1},{129,0},{2,131},{3,130},{130,3},{131,2},{4... | collective-permute-start | bytes 98312 | tf_op jit(solution)/shard_map/ppermute | solution.py:384
  72.8 2.1 %collective-permute-done.6 = f32[2,64,64]{2,1,0:T(8,128)S(1)} collective-permute-done((f32[2,64,64]{2,1,0:T(8,128)S(1)}, f32[2,64,64]{2,1,0:T(8,128)S(1)}, u32[]{:S(2)}, u32[]{:S(2)}) %collective-permute-start.6) | collective-permute-done | bytes 32800 | tf_op jit(solution)/shard_map/ppermute | solution.py:384
  74.9 1.6 collective-permute-start.13
  76.5 3.0 %collective-permute-start.14 = (bf16[512,512]{1,0:T(8,128)(2,1)S(1)}, bf16[512,512]{1,0:T(8,128)(2,1)S(1)}, u32[]{:S(2)}, u32[]{:S(2)}) collective-permute-start(bf16[512,512]{1,0:T(8,128)(2,1)S(1)} %collective-permute-done.12.refs_5_.refs_6_), channel_id=1, source_target_pairs={{0,16},{16,0},{1,17},{17,1},{2,18},{18,2},{3,19},{19,3},{4,20},{20... | collective-permute-start | bytes 1572872 | tf_op jit(solution)/shard_map/ppermute | solution.py:38
  79.4 3.0 %collective-permute-start.27 = (bf16[512,512]{1,0:T(8,128)(2,1)}, bf16[512,512]{1,0:T(8,128)(2,1)S(1)}, u32[]{:S(2)}, u32[]{:S(2)}) collective-permute-start(bf16[512,512]{1,0:T(8,128)(2,1)} %collective-permute-done.26), channel_id=1, source_target_pairs={{0,2},{2,4},{4,6},{6,8},{8,10},{10,12},{12,14},{14,0},{16,30},{18,... | collective-permute-start | bytes 1572872 | tf_op jit(solution)/shard_map/ppermute | solution.py:34
  82.5 2.8 %collective-permute-start.24 = (bf16[512,512]{1,0:T(8,128)(2,1)S(1)}, bf16[512,512]{1,0:T(8,128)(2,1)}, u32[]{:S(2)}, u32[]{:S(2)}) collective-permute-start(bf16[512,512]{1,0:T(8,128)(2,1)S(1)} %collective-permute-done.20.refs_13_.refs_14_), channel_id=1, source_target_pairs={{0,32},{32,64},{64,96},{96,0},{16,112},{48,16},{80,48},{112,80},{1... | collective-permute-start | bytes 1572872 | tf_op jit(solution)/shard_map/ppermute | solution.py:34
  85.4 0.8 copy-done.13
  86.2 0.9 collective-permute-start.8
  87.0 1.9 %collective-permute-done.27.refs_20_ = bf16[512,512]{1,0:T(8,128)(2,1)S(1)} collective-permute-done((bf16[512,512]{1,0:T(8,128)(2,1)}, bf16[512,512]{1,0:T(8,128)(2,1)S(1)}, u32[]{:S(2)}, u32[]{:S(2)}) %collective-permute-start.27) | collective-permute-done | bytes 524320 | tf_op jit(solution)/shard_map/ppermute | solution.py:34
  88.9 3.2 %collective-permute-start.9 = (f32[2,64,64]{2,1,0:T(8,128)S(1)}, f32[2,64,64]{2,1,0:T(8,128)S(1)}, u32[]{:S(2)}, u32[]{:S(2)}) collective-permute-start(f32[2,64,64]{2,1,0:T(8,128)S(1)} %add_add_fusion.1), channel_id=1, source_target_pairs={{0,6},{2,4},{4,2},{6,0},{1,7},{3,5},{5,3},{7,1},{8,14},{10,12},{12... | collective-permute-start | bytes 98312 | tf_op jit(solution)/shard_map/ppermute | solution.py:384
  92.2 1.9 %collective-permute-start.21 = (bf16[512,512]{1,0:T(8,128)(2,1)S(1)}, bf16[512,512]{1,0:T(8,128)(2,1)}, u32[]{:S(2)}, u32[]{:S(2)}) collective-permute-start(bf16[512,512]{1,0:T(8,128)(2,1)S(1)} %collective-permute-done.19.refs_12_.refs_13_), channel_id=1, source_target_pairs={{0,32},{32,64},{64,96},{96,0},{16,112},{48,16},{80,48},{112,80},{1... | collective-permute-start | bytes 1572872 | tf_op jit(solution)/shard_map/ppermute | solution.py:34
  94.0 0.8 copy-done.7
  94.9 3.4 %collective-permute-start.22 = (bf16[512,512]{1,0:T(8,128)(2,1)S(1)}, bf16[512,512]{1,0:T(8,128)(2,1)S(1)}, u32[]{:S(2)}, u32[]{:S(2)}) collective-permute-start(bf16[512,512]{1,0:T(8,128)(2,1)S(1)} %collective-permute-done.20.refs_13_.refs_14_), channel_id=1, source_target_pairs={{0,16},{16,0},{1,17},{17,1},{2,18},{18,2},{3,19},{19,3},{4,20},{20... | collective-permute-start | bytes 1572872 | tf_op jit(solution)/shard_map/ppermute | solution.py:38
  98.2 0.8 copy-done.4
  99.0 0.9 collective-permute-start.29
  100.0 0.8 copy-done.10
  100.8 2.8 %collective-permute-start.36 = (bf16[1024,512]{1,0:T(8,128)(2,1)}, bf16[1024,512]{1,0:T(8,128)(2,1)S(1)}, u32[]{:S(2)}, u32[]{:S(2)}) collective-permute-start(bf16[1024,512]{1,0:T(8,128)(2,1)} %collective-permute-done.35.refs_29_), channel_id=1, source_target_pairs={{0,2},{2,4},{4,6},{6,8},{8,10},{10,12},{12,14},{14,0},{16,30},{18,... | collective-permute-start | bytes 3145736 | tf_op jit(solution)/shard_map/ppermute | solution.py:34
  103.6 1.7 %collective-permute-start.15 = (bf16[512,512]{1,0:T(8,128)(2,1)}, bf16[512,512]{1,0:T(8,128)(2,1)}, u32[]{:S(2)}, u32[]{:S(2)}) collective-permute-start(bf16[512,512]{1,0:T(8,128)(2,1)} %collective-permute-done.13.refs_6_.refs_7_), channel_id=1, source_target_pairs={{0,16},{16,0},{1,17},{17,1},{2,18},{18,2},{3,19},{19,3},{4,20},{20... | collective-permute-start | bytes 1572872 | tf_op jit(solution)/shard_map/ppermute | solution.py:38
  105.3 0.8 copy-done.16
  106.1 1.3 collective-permute-done.29.refs_22_
  107.5 1.8 %collective-permute-start.31 = (bf16[512,512]{1,0:T(8,128)(2,1)}, bf16[512,512]{1,0:T(8,128)(2,1)}, u32[]{:S(2)}, u32[]{:S(2)}) collective-permute-start(bf16[512,512]{1,0:T(8,128)(2,1)} %collective-permute-done.29.refs_22_), channel_id=1, source_target_pairs={{0,2},{2,4},{4,6},{6,8},{8,10},{10,12},{12,14},{14,0},{16,30},{18,... | collective-permute-start | bytes 1572872 | tf_op jit(solution)/shard_map/ppermute | solution.py:34
  109.3 0.8 copy-done.19
  110.1 1.0 collective-permute-start.23
  111.2 1.5 collective-permute-start.30
  112.6 11.7 %collective-permute-done.31.refs_24_ = bf16[512,512]{1,0:T(8,128)(2,1)} collective-permute-done((bf16[512,512]{1,0:T(8,128)(2,1)}, bf16[512,512]{1,0:T(8,128)(2,1)}, u32[]{:S(2)}, u32[]{:S(2)}) %collective-permute-start.31) | collective-permute-done | bytes 524320 | tf_op jit(solution)/shard_map/ppermute | solution.py:34
  124.3 4.5 %inverses.1.refs_2_ = bf16[2,64,64]{2,1,0:T(8,128)(2,1)S(1)} custom-call(f32[2,64,64]{2,1,0:T(8,128)S(1)} %add_add_fusion.refs_0_), custom_call_target="tpu_custom_call" | custom-call | flops 100000000 | bytes 1048576 | tf_op jit(solution)/shard_map/inverses/pallas_call | solution.py:86
  128.9 3.2 %collective-permute-start.10 = (bf16[2,64,64]{2,1,0:T(8,128)(2,1)S(1)}, bf16[2,64,64]{2,1,0:T(8,128)(2,1)S(1)}, u32[]{:S(2)}, u32[]{:S(2)}) collective-permute-start(bf16[2,64,64]{2,1,0:T(8,128)(2,1)S(1)} %inverses.1.refs_2_), channel_id=1, source_target_pairs={{0,8},{8,0},{1,9},{9,1},{2,10},{10,2},{3,11},{11,3},{4,12},{12,4},... | collective-permute-start | bytes 49160 | tf_op jit(solution)/shard_map/ppermute | solution.py:38
  132.1 2.9 %collective-permute-start.37 = (bf16[1024,512]{1,0:T(8,128)(2,1)S(1)}, bf16[1024,512]{1,0:T(8,128)(2,1)S(1)}, u32[]{:S(2)}, u32[]{:S(2)}) collective-permute-start(bf16[1024,512]{1,0:T(8,128)(2,1)S(1)} %collective-permute-done.36.near_ref), channel_id=1, source_target_pairs={{0,2},{2,4},{4,6},{6,8},{8,10},{10,12},{12,14},{14,0},{16,30},{18,... | collective-permute-start | bytes 3145736 | tf_op jit(solution)/shard_map/ppermute | solution.py:34
  135.0 1.0 copy-done.2
  136.0 1.0 copy-done.5
  137.1 1.0 copy-done.8
  138.1 1.0 copy-done.11
  139.1 1.0 copy-done.14
  140.2 1.0 copy-done.17
  141.2 1.0 copy-done.20
  142.3 6.1 %condition_first.1.refs_3_ = bf16[64,64,512]{2,1,0:T(8,128)(2,1)S(1)} custom-call(s32[1]{0:T(128)} %bitcast.refs_0_, s32[1]{0:T(128)} %bitcast.1.refs_1_, bf16[2,64,64]{2,1,0:T(8,128)(2,1)S(1)} %inverses.1.refs_2_, bf16[512,512]{1,0:T(8,128)(2,1)S(1)} %bitcast.7, bf16[512,512]{1,0:T(8,128)(2,1)S(1)} %copy-done.2, ...), custom_call_target="tpu_custom_call" | custom-call | flops 3000000000 | bytes 8388608 | tf_op jit(solution)/shard_map/condition_first/pallas_call | solution.py:175
  148.5 10.7 %condition_and_score.1 = (bf16[512,512]{1,0:T(8,128)(2,1)S(1)}, f32[512,512]{1,0:T(8,128)S(1)}, bf16[4,8,64,512]{3,2,1,0:T(8,128)(2,1)S(1)}) custom-call(s32[1]{0:T(128)} %bitcast.refs_0_, s32[1]{0:T(128)} %bitcast.1.refs_1_, bf16[2,64,64]{2,1,0:T(8,128)(2,1)S(1)} %collective-permute-done.10.refs_2_, bf16[64,64,512]{2,1,0:T(8,128)(2,1)S(1)} %condition_first.1.refs_3_, ...), custom_call_target="tpu_custom_call" | custom-call | flops 6000000000 | bytes 18874368 | tf_op jit(solution)/shard_map/condition_and_score/pallas_call | solution.py:328
  159.3 1.3 collective-permute-start.38
  160.6 1.2 score_own.1
  162.1 1.1 add_multiply_fusion
  (83 shorter events, 0.8 us)
Async XLA Ops:
  0.0 25.9 %copy-start.26 = (bf16[512,512]{1,0:T(8,128)(2,1)S(1)}, bf16[512,512]{1,0:T(8,128)(2,1)}, u32[]{:S(2)}) copy-start(bf16[512,512]{1,0:T(8,128)(2,1)} %param.3) | copy-start | bytes 1572868
  0.0 15.8 %collective-permute-start.33 = (bf16[512,512]{1,0:T(8,128)(2,1)}, bf16[512,512]{1,0:T(8,128)(2,1)S(1)}, u32[]{:S(2)}, u32[]{:S(2)}) collective-permute-start(bf16[512,512]{1,0:T(8,128)(2,1)} %refs_26_.1), channel_id=1, source_target_pairs={{0,1},{1,0},{2,3},{3,2},{4,5},{5,4},{6,7},{7,6},{8,9},{9,8},{10,11... | collective-permute-start | bytes 1572872 | tf_op jit(solution)/shard_map/ppermute | solution.py:38
  2.0 29.7 %copy-start = (bf16[512,512]{1,0:T(8,128)(2,1)S(1)}, bf16[512,512]{1,0:T(8,128)(2,1)}, u32[]{:S(2)}) copy-start(bf16[512,512]{1,0:T(8,128)(2,1)} %refs_26_.1) | copy-start | bytes 1572868
  2.0 30.7 %all-to-all-start = ((bf16[8,64,512]{2,1,0:T(8,128)(2,1)}), bf16[8,64,512]{2,1,0:T(8,128)(2,1)S(1)}, u32[]{:S(2)}, u32[]{:S(2)}) async-start(bf16[8,64,512]{2,1,0:T(8,128)(2,1)} %bitcast.9), calls=%async_computation | async-start | bytes 1048576 | tf_op jit(solution)/shard_map/all_to_all | solution.py:392
  15.8 2.3 %copy-start.22 = (bf16[512,512]{1,0:T(8,128)(2,1)}, bf16[512,512]{1,0:T(8,128)(2,1)S(1)}, u32[]{:S(2)}) copy-start(bf16[512,512]{1,0:T(8,128)(2,1)S(1)} %collective-permute-done.33.refs_27_) | copy-start | bytes 1572868
  18.1 41.3 %collective-permute-start.34 = (bf16[1024,512]{1,0:T(8,128)(2,1)}, bf16[1024,512]{1,0:T(8,128)(2,1)}, u32[]{:S(2)}, u32[]{:S(2)}) collective-permute-start(bf16[1024,512]{1,0:T(8,128)(2,1)} %pad_maximum_fusion), channel_id=1, source_target_pairs={{0,2},{2,4},{4,6},{6,8},{8,10},{10,12},{12,14},{14,0},{16,30},{18,... | collective-permute-start | bytes 3145736 | tf_op jit(solution)/shard_map/ppermute | solution.py:34
  26.1 13.6 %collective-permute-start.18 = (bf16[512,512]{1,0:T(8,128)(2,1)S(1)}, bf16[512,512]{1,0:T(8,128)(2,1)S(1)}, u32[]{:S(2)}, u32[]{:S(2)}) collective-permute-start(bf16[512,512]{1,0:T(8,128)(2,1)S(1)} %bitcast.4), channel_id=1, source_target_pairs={{0,128},{128,0},{1,129},{129,1},{2,130},{130,2},{3,131},{131,3},{4... | collective-permute-start | bytes 1572872 | tf_op jit(solution)/shard_map/ppermute | solution.py:38
  29.0 10.7 %collective-permute-start.12 = (bf16[512,512]{1,0:T(8,128)(2,1)S(1)}, bf16[512,512]{1,0:T(8,128)(2,1)S(1)}, u32[]{:S(2)}, u32[]{:S(2)}) collective-permute-start(bf16[512,512]{1,0:T(8,128)(2,1)S(1)} %bitcast.5), channel_id=1, source_target_pairs={{0,32},{32,64},{64,96},{96,0},{16,112},{48,16},{80,48},{112,80},{1... | collective-permute-start | bytes 1572872 | tf_op jit(solution)/shard_map/ppermute | solution.py:34
  31.7 10.8 %collective-permute-start.11 = (bf16[512,512]{1,0:T(8,128)(2,1)S(1)}, bf16[512,512]{1,0:T(8,128)(2,1)S(1)}, u32[]{:S(2)}, u32[]{:S(2)}) collective-permute-start(bf16[512,512]{1,0:T(8,128)(2,1)S(1)} %bitcast.6), channel_id=1, source_target_pairs={{0,16},{16,0},{1,17},{17,1},{2,18},{18,2},{3,19},{19,3},{4,20},{20... | collective-permute-start | bytes 1572872 | tf_op jit(solution)/shard_map/ppermute | solution.py:38
  31.7 30.1 %collective-permute-start.26 = (bf16[512,512]{1,0:T(8,128)(2,1)S(1)}, bf16[512,512]{1,0:T(8,128)(2,1)}, u32[]{:S(2)}, u32[]{:S(2)}) collective-permute-start(bf16[512,512]{1,0:T(8,128)(2,1)S(1)} %copy-done), channel_id=1, source_target_pairs={{0,16},{16,0},{1,17},{17,1},{2,18},{18,2},{3,19},{19,3},{4,20},{20... | collective-permute-start | bytes 1572872 | tf_op jit(solution)/shard_map/ppermute | solution.py:38
  39.7 2.7 %collective-permute-start = (f32[2,64,64]{2,1,0:T(8,128)S(1)}, f32[2,64,64]{2,1,0:T(8,128)S(1)}, u32[]{:S(2)}, u32[]{:S(2)}) collective-permute-start(f32[2,64,64]{2,1,0:T(8,128)S(1)} %factor_terms.1), channel_id=1, source_target_pairs={{0,16},{16,0},{1,17},{17,1},{2,18},{18,2},{3,19},{19,3},{4,20},{20... | collective-permute-start | bytes 98312 | tf_op jit(solution)/shard_map/ppermute | solution.py:384
  39.7 36.8 %collective-permute-start.20 = (bf16[512,512]{1,0:T(8,128)(2,1)S(1)}, bf16[512,512]{1,0:T(8,128)(2,1)S(1)}, u32[]{:S(2)}, u32[]{:S(2)}) collective-permute-start(bf16[512,512]{1,0:T(8,128)(2,1)S(1)} %collective-permute-done.18.refs_11_.refs_12_), channel_id=1, source_target_pairs={{0,32},{32,64},{64,96},{96,0},{16,112},{48,16},{80,48},{112,80},{1... | collective-permute-start | bytes 1572872 | tf_op jit(solution)/shard_map/ppermute | solution.py:34
  42.4 37.0 %collective-permute-start.19 = (bf16[512,512]{1,0:T(8,128)(2,1)S(1)}, bf16[512,512]{1,0:T(8,128)(2,1)S(1)}, u32[]{:S(2)}, u32[]{:S(2)}) collective-permute-start(bf16[512,512]{1,0:T(8,128)(2,1)S(1)} %collective-permute-done.18.refs_11_.refs_12_), channel_id=1, source_target_pairs={{0,16},{16,0},{1,17},{17,1},{2,18},{18,2},{3,19},{19,3},{4,20},{20... | collective-permute-start | bytes 1572872 | tf_op jit(solution)/shard_map/ppermute | solution.py:38
  42.5 57.5 %copy-start.1 = (bf16[512,512]{1,0:T(8,128)(2,1)}, bf16[512,512]{1,0:T(8,128)(2,1)S(1)}, u32[]{:S(2)}) copy-start(bf16[512,512]{1,0:T(8,128)(2,1)S(1)} %collective-permute-done.11.refs_4_.refs_5_) | copy-start | bytes 1572868
  42.5 7.0 %collective-permute-start.1 = (f32[2,64,64]{2,1,0:T(8,128)S(1)}, f32[2,64,64]{2,1,0:T(8,128)S(1)}, u32[]{:S(2)}, u32[]{:S(2)}) collective-permute-start(f32[2,64,64]{2,1,0:T(8,128)S(1)} %add.53), channel_id=1, source_target_pairs={{0,32},{32,0},{64,96},{96,64},{1,33},{33,1},{65,97},{97,65},{2,34}... | collective-permute-start | bytes 98312 | tf_op jit(solution)/shard_map/ppermute | solution.py:384
  49.4 4.6 %collective-permute-start.2 = (f32[2,64,64]{2,1,0:T(8,128)S(1)}, f32[2,64,64]{2,1,0:T(8,128)S(1)}, u32[]{:S(2)}, u32[]{:S(2)}) collective-permute-start(f32[2,64,64]{2,1,0:T(8,128)S(1)} %add.53), channel_id=1, source_target_pairs={{0,64},{32,96},{64,0},{96,32},{1,65},{33,97},{65,1},{97,33},{2,66}... | collective-permute-start | bytes 98312 | tf_op jit(solution)/shard_map/ppermute | solution.py:384
  54.1 4.3 %collective-permute-start.3 = (f32[2,64,64]{2,1,0:T(8,128)S(1)}, f32[2,64,64]{2,1,0:T(8,128)S(1)}, u32[]{:S(2)}, u32[]{:S(2)}) collective-permute-start(f32[2,64,64]{2,1,0:T(8,128)S(1)} %add.53), channel_id=1, source_target_pairs={{0,96},{32,64},{64,32},{96,0},{1,97},{33,65},{65,33},{97,1},{2,98}... | collective-permute-start | bytes 98312 | tf_op jit(solution)/shard_map/ppermute | solution.py:384
  58.4 24.1 %collective-permute-start.16 = (bf16[512,512]{1,0:T(8,128)(2,1)S(1)}, bf16[512,512]{1,0:T(8,128)(2,1)S(1)}, u32[]{:S(2)}, u32[]{:S(2)}) collective-permute-start(bf16[512,512]{1,0:T(8,128)(2,1)S(1)} %collective-permute-done.12.refs_5_.refs_6_), channel_id=1, source_target_pairs={{0,32},{32,64},{64,96},{96,0},{16,112},{48,16},{80,48},{112,80},{1... | collective-permute-start | bytes 1572872 | tf_op jit(solution)/shard_map/ppermute | solution.py:34
  59.4 41.4 %collective-permute-start.35 = (bf16[1024,512]{1,0:T(8,128)(2,1)}, bf16[1024,512]{1,0:T(8,128)(2,1)}, u32[]{:S(2)}, u32[]{:S(2)}) collective-permute-start(bf16[1024,512]{1,0:T(8,128)(2,1)} %collective-permute-done.34.refs_28_), channel_id=1, source_target_pairs={{0,2},{2,4},{4,6},{6,8},{8,10},{10,12},{12,14},{14,0},{16,30},{18,... | collective-permute-start | bytes 3145736 | tf_op jit(solution)/shard_map/ppermute | solution.py:34
  61.8 3.7 %collective-permute-start.4 = (f32[2,64,64]{2,1,0:T(8,128)S(1)}, f32[2,64,64]{2,1,0:T(8,128)S(1)}, u32[]{:S(2)}, u32[]{:S(2)}) collective-permute-start(f32[2,64,64]{2,1,0:T(8,128)S(1)} %add_add_fusion.2), channel_id=1, source_target_pairs={{0,1},{1,0},{128,129},{129,128},{2,3},{3,2},{130,131},{131,130},{4... | collective-permute-start | bytes 98312 | tf_op jit(solution)/shard_map/ppermute | solution.py:384
  65.4 4.6 %collective-permute-start.5 = (f32[2,64,64]{2,1,0:T(8,128)S(1)}, f32[2,64,64]{2,1,0:T(8,128)S(1)}, u32[]{:S(2)}, u32[]{:S(2)}) collective-permute-start(f32[2,64,64]{2,1,0:T(8,128)S(1)} %add_add_fusion.2), channel_id=1, source_target_pairs={{0,128},{1,129},{128,0},{129,1},{2,130},{3,131},{130,2},{131,3},{4... | collective-permute-start | bytes 98312 | tf_op jit(solution)/shard_map/ppermute | solution.py:384
  70.1 4.8 %collective-permute-start.6 = (f32[2,64,64]{2,1,0:T(8,128)S(1)}, f32[2,64,64]{2,1,0:T(8,128)S(1)}, u32[]{:S(2)}, u32[]{:S(2)}) collective-permute-start(f32[2,64,64]{2,1,0:T(8,128)S(1)} %add_add_fusion.2), channel_id=1, source_target_pairs={{0,129},{1,128},{128,1},{129,0},{2,131},{3,130},{130,3},{131,2},{4... | collective-permute-start | bytes 98312 | tf_op jit(solution)/shard_map/ppermute | solution.py:384
  74.9 10.4 %collective-permute-start.13 = (bf16[512,512]{1,0:T(8,128)(2,1)S(1)}, bf16[512,512]{1,0:T(8,128)(2,1)}, u32[]{:S(2)}, u32[]{:S(2)}) collective-permute-start(bf16[512,512]{1,0:T(8,128)(2,1)S(1)} %collective-permute-done.11.refs_4_.refs_5_), channel_id=1, source_target_pairs={{0,32},{32,64},{64,96},{96,0},{16,112},{48,16},{80,48},{112,80},{1... | collective-permute-start | bytes 1572872 | tf_op jit(solution)/shard_map/ppermute | solution.py:34
  76.5 8.9 %collective-permute-start.14 = (bf16[512,512]{1,0:T(8,128)(2,1)S(1)}, bf16[512,512]{1,0:T(8,128)(2,1)S(1)}, u32[]{:S(2)}, u32[]{:S(2)}) collective-permute-start(bf16[512,512]{1,0:T(8,128)(2,1)S(1)} %collective-permute-done.12.refs_5_.refs_6_), channel_id=1, source_target_pairs={{0,16},{16,0},{1,17},{17,1},{2,18},{18,2},{3,19},{19,3},{4,20},{20... | collective-permute-start | bytes 1572872 | tf_op jit(solution)/shard_map/ppermute | solution.py:38
  79.4 9.5 %collective-permute-start.27 = (bf16[512,512]{1,0:T(8,128)(2,1)}, bf16[512,512]{1,0:T(8,128)(2,1)S(1)}, u32[]{:S(2)}, u32[]{:S(2)}) collective-permute-start(bf16[512,512]{1,0:T(8,128)(2,1)} %collective-permute-done.26), channel_id=1, source_target_pairs={{0,2},{2,4},{4,6},{6,8},{8,10},{10,12},{12,14},{14,0},{16,30},{18,... | collective-permute-start | bytes 1572872 | tf_op jit(solution)/shard_map/ppermute | solution.py:34
  82.5 17.5 %collective-permute-start.24 = (bf16[512,512]{1,0:T(8,128)(2,1)S(1)}, bf16[512,512]{1,0:T(8,128)(2,1)}, u32[]{:S(2)}, u32[]{:S(2)}) collective-permute-start(bf16[512,512]{1,0:T(8,128)(2,1)S(1)} %collective-permute-done.20.refs_13_.refs_14_), channel_id=1, source_target_pairs={{0,32},{32,64},{64,96},{96,0},{16,112},{48,16},{80,48},{112,80},{1... | collective-permute-start | bytes 1572872 | tf_op jit(solution)/shard_map/ppermute | solution.py:34
  85.3 6.9 %collective-permute-start.7 = (f32[2,64,64]{2,1,0:T(8,128)S(1)}, f32[2,64,64]{2,1,0:T(8,128)S(1)}, u32[]{:S(2)}, u32[]{:S(2)}) collective-permute-start(f32[2,64,64]{2,1,0:T(8,128)S(1)} %add_add_fusion.1), channel_id=1, source_target_pairs={{0,2},{2,0},{4,6},{6,4},{1,3},{3,1},{5,7},{7,5},{8,10},{10,8},{12,... | collective-permute-start | bytes 98312 | tf_op jit(solution)/shard_map/ppermute | solution.py:384
  86.2 8.7 %collective-permute-start.8 = (f32[2,64,64]{2,1,0:T(8,128)S(1)}, f32[2,64,64]{2,1,0:T(8,128)S(1)}, u32[]{:S(2)}, u32[]{:S(2)}) collective-permute-start(f32[2,64,64]{2,1,0:T(8,128)S(1)} %add_add_fusion.1), channel_id=1, source_target_pairs={{0,4},{2,6},{4,0},{6,2},{1,5},{3,7},{5,1},{7,3},{8,12},{10,14},{12... | collective-permute-start | bytes 98312 | tf_op jit(solution)/shard_map/ppermute | solution.py:384
  88.9 20.4 %copy-start.24 = (bf16[512,512]{1,0:T(8,128)(2,1)}, bf16[512,512]{1,0:T(8,128)(2,1)S(1)}, u32[]{:S(2)}) copy-start(bf16[512,512]{1,0:T(8,128)(2,1)S(1)} %collective-permute-done.27.refs_20_) | copy-start | bytes 1572868
  88.9 10.1 %collective-permute-start.9 = (f32[2,64,64]{2,1,0:T(8,128)S(1)}, f32[2,64,64]{2,1,0:T(8,128)S(1)}, u32[]{:S(2)}, u32[]{:S(2)}) collective-permute-start(f32[2,64,64]{2,1,0:T(8,128)S(1)} %add_add_fusion.1), channel_id=1, source_target_pairs={{0,6},{2,4},{4,2},{6,0},{1,7},{3,5},{5,3},{7,1},{8,14},{10,12},{12... | collective-permute-start | bytes 98312 | tf_op jit(solution)/shard_map/ppermute | solution.py:384
  92.2 11.5 %collective-permute-start.21 = (bf16[512,512]{1,0:T(8,128)(2,1)S(1)}, bf16[512,512]{1,0:T(8,128)(2,1)}, u32[]{:S(2)}, u32[]{:S(2)}) collective-permute-start(bf16[512,512]{1,0:T(8,128)(2,1)S(1)} %collective-permute-done.19.refs_12_.refs_13_), channel_id=1, source_target_pairs={{0,32},{32,64},{64,96},{96,0},{16,112},{48,16},{80,48},{112,80},{1... | collective-permute-start | bytes 1572872 | tf_op jit(solution)/shard_map/ppermute | solution.py:34
  94.0 0.8 copy-start.7
  94.9 10.5 %collective-permute-start.22 = (bf16[512,512]{1,0:T(8,128)(2,1)S(1)}, bf16[512,512]{1,0:T(8,128)(2,1)S(1)}, u32[]{:S(2)}, u32[]{:S(2)}) collective-permute-start(bf16[512,512]{1,0:T(8,128)(2,1)S(1)} %collective-permute-done.20.refs_13_.refs_14_), channel_id=1, source_target_pairs={{0,16},{16,0},{1,17},{17,1},{2,18},{18,2},{3,19},{19,3},{4,20},{20... | collective-permute-start | bytes 1572872 | tf_op jit(solution)/shard_map/ppermute | solution.py:38
  99.0 8.4 %collective-permute-start.29 = (bf16[512,512]{1,0:T(8,128)(2,1)S(1)}, bf16[512,512]{1,0:T(8,128)(2,1)}, u32[]{:S(2)}, u32[]{:S(2)}) collective-permute-start(bf16[512,512]{1,0:T(8,128)(2,1)S(1)} %collective-permute-done.27.refs_20_), channel_id=1, source_target_pairs={{0,2},{2,4},{4,6},{6,8},{8,10},{10,12},{12,14},{14,0},{16,30},{18,... | collective-permute-start | bytes 1572872 | tf_op jit(solution)/shard_map/ppermute | solution.py:34
  99.9 9.3 %collective-permute-start.17 = (bf16[512,512]{1,0:T(8,128)(2,1)S(1)}, bf16[512,512]{1,0:T(8,128)(2,1)S(1)}, u32[]{:S(2)}, u32[]{:S(2)}) collective-permute-start(bf16[512,512]{1,0:T(8,128)(2,1)S(1)} %collective-permute-done.16.refs_9_.refs_10_), channel_id=1, source_target_pairs={{0,16},{16,0},{1,17},{17,1},{2,18},{18,2},{3,19},{19,3},{4,20},{20... | collective-permute-start | bytes 1572872 | tf_op jit(solution)/shard_map/ppermute | solution.py:38
  100.0 0.8 copy-start.10
  100.8 31.3 %collective-permute-start.36 = (bf16[1024,512]{1,0:T(8,128)(2,1)}, bf16[1024,512]{1,0:T(8,128)(2,1)S(1)}, u32[]{:S(2)}, u32[]{:S(2)}) collective-permute-start(bf16[1024,512]{1,0:T(8,128)(2,1)} %collective-permute-done.35.refs_29_), channel_id=1, source_target_pairs={{0,2},{2,4},{4,6},{6,8},{8,10},{10,12},{12,14},{14,0},{16,30},{18,... | collective-permute-start | bytes 3145736 | tf_op jit(solution)/shard_map/ppermute | solution.py:34
  103.6 7.6 %collective-permute-start.15 = (bf16[512,512]{1,0:T(8,128)(2,1)}, bf16[512,512]{1,0:T(8,128)(2,1)}, u32[]{:S(2)}, u32[]{:S(2)}) collective-permute-start(bf16[512,512]{1,0:T(8,128)(2,1)} %collective-permute-done.13.refs_6_.refs_7_), channel_id=1, source_target_pairs={{0,16},{16,0},{1,17},{17,1},{2,18},{18,2},{3,19},{19,3},{4,20},{20... | collective-permute-start | bytes 1572872 | tf_op jit(solution)/shard_map/ppermute | solution.py:38
  106.1 5.0 %collective-permute-start.25 = (bf16[512,512]{1,0:T(8,128)(2,1)}, bf16[512,512]{1,0:T(8,128)(2,1)}, u32[]{:S(2)}, u32[]{:S(2)}) collective-permute-start(bf16[512,512]{1,0:T(8,128)(2,1)} %collective-permute-done.24.refs_17_.refs_18_), channel_id=1, source_target_pairs={{0,16},{16,0},{1,17},{17,1},{2,18},{18,2},{3,19},{19,3},{4,20},{20... | collective-permute-start | bytes 1572872 | tf_op jit(solution)/shard_map/ppermute | solution.py:38
  107.5 16.9 %collective-permute-start.31 = (bf16[512,512]{1,0:T(8,128)(2,1)}, bf16[512,512]{1,0:T(8,128)(2,1)}, u32[]{:S(2)}, u32[]{:S(2)}) collective-permute-start(bf16[512,512]{1,0:T(8,128)(2,1)} %collective-permute-done.29.refs_22_), channel_id=1, source_target_pairs={{0,2},{2,4},{4,6},{6,8},{8,10},{10,12},{12,14},{14,0},{16,30},{18,... | collective-permute-start | bytes 1572872 | tf_op jit(solution)/shard_map/ppermute | solution.py:34
  109.3 0.8 copy-start.19
  110.1 18.7 %collective-permute-start.23 = (bf16[512,512]{1,0:T(8,128)(2,1)}, bf16[512,512]{1,0:T(8,128)(2,1)}, u32[]{:S(2)}, u32[]{:S(2)}) collective-permute-start(bf16[512,512]{1,0:T(8,128)(2,1)} %collective-permute-done.21.refs_14_.refs_15_), channel_id=1, source_target_pairs={{0,16},{16,0},{1,17},{17,1},{2,18},{18,2},{3,19},{19,3},{4,20},{20... | collective-permute-start | bytes 1572872 | tf_op jit(solution)/shard_map/ppermute | solution.py:38
  111.2 37.2 %collective-permute-start.28 = (bf16[512,512]{1,0:T(8,128)(2,1)}, bf16[512,512]{1,0:T(8,128)(2,1)}, u32[]{:S(2)}, u32[]{:S(2)}) collective-permute-start(bf16[512,512]{1,0:T(8,128)(2,1)} %copy-done.24), channel_id=1, source_target_pairs={{0,1},{1,0},{2,3},{3,2},{4,5},{5,4},{6,7},{7,6},{8,9},{9,8},{10,11... | collective-permute-start | bytes 1572872 | tf_op jit(solution)/shard_map/ppermute | solution.py:38
  111.2 37.2 %collective-permute-start.30 = (bf16[512,512]{1,0:T(8,128)(2,1)}, bf16[512,512]{1,0:T(8,128)(2,1)}, u32[]{:S(2)}, u32[]{:S(2)}) collective-permute-start(bf16[512,512]{1,0:T(8,128)(2,1)} %collective-permute-done.29.refs_22_), channel_id=1, source_target_pairs={{0,1},{1,0},{2,3},{3,2},{4,5},{5,4},{6,7},{7,6},{8,9},{9,8},{10,11... | collective-permute-start | bytes 1572872 | tf_op jit(solution)/shard_map/ppermute | solution.py:38
  124.3 24.1 %collective-permute-start.32 = (bf16[512,512]{1,0:T(8,128)(2,1)}, bf16[512,512]{1,0:T(8,128)(2,1)}, u32[]{:S(2)}, u32[]{:S(2)}) collective-permute-start(bf16[512,512]{1,0:T(8,128)(2,1)} %collective-permute-done.31.refs_24_), channel_id=1, source_target_pairs={{0,1},{1,0},{2,3},{3,2},{4,5},{5,4},{6,7},{7,6},{8,9},{9,8},{10,11... | collective-permute-start | bytes 1572872 | tf_op jit(solution)/shard_map/ppermute | solution.py:38
  128.9 19.5 %collective-permute-start.10 = (bf16[2,64,64]{2,1,0:T(8,128)(2,1)S(1)}, bf16[2,64,64]{2,1,0:T(8,128)(2,1)S(1)}, u32[]{:S(2)}, u32[]{:S(2)}) collective-permute-start(bf16[2,64,64]{2,1,0:T(8,128)(2,1)S(1)} %inverses.1.refs_2_), channel_id=1, source_target_pairs={{0,8},{8,0},{1,9},{9,1},{2,10},{10,2},{3,11},{11,3},{4,12},{12,4},... | collective-permute-start | bytes 49160 | tf_op jit(solution)/shard_map/ppermute | solution.py:38
  132.1 28.5 %collective-permute-start.37 = (bf16[1024,512]{1,0:T(8,128)(2,1)S(1)}, bf16[1024,512]{1,0:T(8,128)(2,1)S(1)}, u32[]{:S(2)}, u32[]{:S(2)}) collective-permute-start(bf16[1024,512]{1,0:T(8,128)(2,1)S(1)} %collective-permute-done.36.near_ref), channel_id=1, source_target_pairs={{0,2},{2,4},{4,6},{6,8},{8,10},{10,12},{12,14},{14,0},{16,30},{18,... | collective-permute-start | bytes 3145736 | tf_op jit(solution)/shard_map/ppermute | solution.py:34
  135.0 1.0 copy-start.2
  136.0 1.0 copy-start.5
  137.0 1.0 copy-start.8
  138.1 1.0 copy-start.11
  139.1 1.0 copy-start.14
  140.2 1.0 copy-start.17
  141.2 1.0 copy-start.20
  142.3 6.2 %copy-start.3 = (bf16[512,512]{1,0:T(8,128)(2,1)S(1)}, bf16[512,512]{1,0:T(8,128)(2,1)}, u32[]{:S(2)}) copy-start(bf16[512,512]{1,0:T(8,128)(2,1)} %copy-done.1) | copy-start | bytes 1572868
  142.3 6.2 %copy-start.6 = (bf16[512,512]{1,0:T(8,128)(2,1)S(1)}, bf16[512,512]{1,0:T(8,128)(2,1)}, u32[]{:S(2)}) copy-start(bf16[512,512]{1,0:T(8,128)(2,1)} %copy-done.4) | copy-start | bytes 1572868
  142.3 6.2 %copy-start.9 = (bf16[512,512]{1,0:T(8,128)(2,1)S(1)}, bf16[512,512]{1,0:T(8,128)(2,1)}, u32[]{:S(2)}) copy-start(bf16[512,512]{1,0:T(8,128)(2,1)} %copy-done.7) | copy-start | bytes 1572868
  142.3 6.2 %copy-start.12 = (bf16[512,512]{1,0:T(8,128)(2,1)S(1)}, bf16[512,512]{1,0:T(8,128)(2,1)}, u32[]{:S(2)}) copy-start(bf16[512,512]{1,0:T(8,128)(2,1)} %copy-done.10) | copy-start | bytes 1572868
  142.3 6.2 %copy-start.15 = (bf16[512,512]{1,0:T(8,128)(2,1)S(1)}, bf16[512,512]{1,0:T(8,128)(2,1)}, u32[]{:S(2)}) copy-start(bf16[512,512]{1,0:T(8,128)(2,1)} %copy-done.13) | copy-start | bytes 1572868
  142.3 6.2 %copy-start.18 = (bf16[512,512]{1,0:T(8,128)(2,1)S(1)}, bf16[512,512]{1,0:T(8,128)(2,1)}, u32[]{:S(2)}) copy-start(bf16[512,512]{1,0:T(8,128)(2,1)} %copy-done.16) | copy-start | bytes 1572868
  142.3 6.2 %copy-start.21 = (bf16[512,512]{1,0:T(8,128)(2,1)S(1)}, bf16[512,512]{1,0:T(8,128)(2,1)}, u32[]{:S(2)}) copy-start(bf16[512,512]{1,0:T(8,128)(2,1)} %copy-done.19) | copy-start | bytes 1572868
  142.3 6.2 %copy-start.23 = (bf16[512,512]{1,0:T(8,128)(2,1)S(1)}, bf16[512,512]{1,0:T(8,128)(2,1)}, u32[]{:S(2)}) copy-start(bf16[512,512]{1,0:T(8,128)(2,1)} %copy-done.22) | copy-start | bytes 1572868
  142.3 6.2 %copy-start.25 = (bf16[512,512]{1,0:T(8,128)(2,1)S(1)}, bf16[512,512]{1,0:T(8,128)(2,1)}, u32[]{:S(2)}) copy-start(bf16[512,512]{1,0:T(8,128)(2,1)} %copy-done.24) | copy-start | bytes 1572868
  159.3 2.8 %collective-permute-start.38 = (bf16[512,512]{1,0:T(8,128)(2,1)S(1)}, bf16[512,512]{1,0:T(8,128)(2,1)S(1)}, u32[]{:S(2)}, u32[]{:S(2)}) collective-permute-start(bf16[512,512]{1,0:T(8,128)(2,1)S(1)} %get-tuple-element.10), channel_id=1, source_target_pairs={{0,16},{16,0},{1,17},{17,1},{2,18},{18,2},{3,19},{19,3},{4,20},{20... | collective-permute-start | bytes 1572872 | tf_op jit(solution)/shard_map/ppermute | solution.py:38
  (3 other events, 2.4 us)
